TPU v7x, 32 devices: a whole 2x2x4 slice. The times are simulated.
32 devices in a mesh: survey: 4 (over z), tile: 8 (over y, x, core).
Axes of the slice: x: 2, y: 2, z: 4, core: 2. Of those that a mesh axis runs over, the one named last changes fastest.
Arguments:
- data: bfloat16 [4, 64, 128, 256], P('survey', 'tile'), may hold values from -12 to 12
- correlation_index: int32 [4, 8, 4, 128], P(None, 'tile'), may hold values from 0 to 1023, as said below
- correlation_count: int32 [4, 8, 4], P(None, 'tile'), may hold values from 0 to 128, as said below
- smoothing: float32 [3], replicated, may hold values from 0.5 to 4
Outputs:
- fields: float32 [4, 3, 64, 128], P('survey', None, 'tile')
- volume: bfloat16 [4, 64, 128, 256], P('survey', 'tile')
Inputs may be any that keep to these rules, and one draw needn't show every extreme that they name: `correlation_index`: each list holds 128 consecutive positions of the tile. `correlation_count`: zero where s equals p; one or more where s is p + 1 modulo 4; in every draw one tile and one destination group receive 128 live slots from every other group.
All inputs are finite; a program needn't handle non-finite values.
Results may differ from a plain program's by a relative error of at most 0.0014.
Values may be sent and summed in bfloat16 or wider, within the bound.
No kernel may reach another device: no remote copies, remote signals or barrier semaphores. Data moves between devices by JAX's collectives and lax.ppermute only.
A program may use at most 64 MiB of HBM per device.

v0:
```python
import jax
import jax.numpy as jnp
from jax import lax
from jax.sharding import PartitionSpec as P

ROUNDS = 2
CG_ITERS = 3


damping = 0.05
sim_eps = 1e-05


def extended(array, sides, width):
    for axis, dim in sides:
        devices, length = (lax.axis_size(axis), array.shape[dim])
        up = [(i, (i + 1) % devices) for i in range(devices - 1)]
        down = [(j, i) for i, j in up]
        last = lax.slice_in_dim(array, length - width, length, axis=dim)
        leading = lax.slice_in_dim(array, 0, width, axis=dim)
        before = lax.ppermute(last, axis, up)
        after = lax.ppermute(leading, axis, down)
        array = jnp.concatenate([before, array, after], axis=dim)
    return array


def time_axis(samples):
    return (jnp.arange(samples, dtype=jnp.float32) - (samples - 1) / 2.0) / (samples / 2.0)


def time_slope(trace_rows):
    padded = jnp.pad(trace_rows, [(0, 0)] * (trace_rows.ndim - 1) + [(1, 1)])
    return 0.5 * (padded[..., 2:] - padded[..., :-2])


def corrected(raw_rows, time_shift, log_gain, gain_trend):
    values = raw_rows.astype(jnp.float32)
    time_pos = time_axis(raw_rows.shape[-1])
    amplitude = jnp.exp(log_gain[..., None] + gain_trend[..., None] * time_pos)
    return (amplitude * (values + time_shift[..., None] * time_slope(values))).astype(jnp.bfloat16)


def pair_terms(own_rows, partner_rows, live_mask):
    own_vals = own_rows.astype(jnp.float32)
    partner_vals = partner_rows.astype(jnp.float32)
    time_pos = time_axis(own_vals.shape[-1])
    residual = partner_vals - own_vals
    moved = time_slope(own_vals)
    tilted = time_pos * own_vals
    energy = jnp.mean(own_vals * own_vals, axis=-1)
    cross_term = jnp.mean(own_vals * partner_vals, axis=-1)
    other_energy = jnp.mean(partner_vals * partner_vals, axis=-1)
    weight = live_mask * cross_term * cross_term / ((energy + sim_eps) * (other_energy + sim_eps))
    numerator = jnp.stack(
        [
            jnp.mean(residual * moved, axis=-1),
            jnp.mean(residual * own_vals, axis=-1),
            jnp.mean(residual * tilted, axis=-1),
        ]
    )
    denominator = jnp.stack(
        [jnp.mean(moved * moved, axis=-1), energy, jnp.mean(tilted * tilted, axis=-1)]
    )
    return (weight * numerator, weight * denominator)


def send_traces(current, send_index):
    outgoing = jnp.take(current, send_index, axis=0)
    return lax.all_to_all(outgoing, "survey", split_axis=0, concat_axis=0, tiled=True)


def smooth_apply(field, weights, strength):
    padded = extended(field, (("tile", 1),), 1)
    padded = jnp.pad(padded, ((0, 0), (0, 0), (1, 1)))
    beside = padded[:, 2:, 1:-1] + padded[:, :-2, 1:-1] + padded[:, 1:-1, 2:] + padded[:, 1:-1, :-2]
    return (weights + damping + 4.0 * strength) * field - strength * beside


def paired(residual, image):
    return lax.psum(
        (jnp.sum(residual * residual, axis=(1, 2)), jnp.sum(residual * image, axis=(1, 2))), "tile"
    )


def conjugate(target, weights, strength):
    solution = jnp.zeros_like(target)
    residual = target
    image = smooth_apply(residual, weights, strength)
    norm_now, product = paired(residual, image)
    alpha = norm_now / product
    direction, along = (residual, image)
    for iteration in range(CG_ITERS):
        solution = solution + alpha[:, None, None] * direction
        residual = residual - alpha[:, None, None] * along
        if iteration + 1 < CG_ITERS:
            image = smooth_apply(residual, weights, strength)
            norm_next, product = paired(residual, image)
            ratio = norm_next / norm_now
            alpha = norm_next / (product - ratio * norm_next / alpha)
            direction = residual + ratio[:, None, None] * direction
            along = image + ratio[:, None, None] * along
            norm_now = norm_next
    return solution


def solve_round(current, partner_rows, recv_index, live_mask, strength, rows_x, rows_y):
    own_rows = jnp.take(current, recv_index, axis=0)
    numerator, denominator = pair_terms(own_rows, partner_rows, live_mask)
    empty_sum = jnp.zeros((3, rows_x * rows_y), jnp.float32)
    target = empty_sum.at[:, recv_index].add(numerator).reshape(3, rows_x, rows_y)
    weights = empty_sum.at[:, recv_index].add(denominator).reshape(3, rows_x, rows_y)
    update = conjugate(target, weights, strength)
    return update.reshape(3, rows_x * rows_y)


def local(data, correlation_index, correlation_count, smoothing):
    own_group = lax.axis_index("survey")
    rows_x, rows_y, samples = (data.shape[1], data.shape[2], data.shape[3])
    flat_data = data.reshape(rows_x * rows_y, samples)
    index_here = correlation_index[:, 0]
    count_here = correlation_count[:, 0]
    send_index = lax.dynamic_index_in_dim(index_here, own_group, axis=0, keepdims=False)
    recv_index = lax.dynamic_index_in_dim(index_here, own_group, axis=1, keepdims=False)
    recv_count = lax.dynamic_index_in_dim(count_here, own_group, axis=1, keepdims=False)
    slot_ids = jnp.arange(index_here.shape[2], dtype=jnp.int32)
    live_mask = (slot_ids[None, :] < recv_count[:, None]).astype(jnp.float32)
    strength = smoothing[:, None, None]
    fields = jnp.zeros((3, rows_x * rows_y), jnp.float32)
    for outer_round in range(ROUNDS):
        current = corrected(flat_data, fields[0], fields[1], fields[2])
        partner_rows = send_traces(current, send_index)
        fields = fields + solve_round(
            current, partner_rows, recv_index, live_mask, strength, rows_x, rows_y
        )
    volume = corrected(flat_data, fields[0], fields[1], fields[2])
    return (fields.reshape(1, 3, rows_x, rows_y), volume.reshape(1, rows_x, rows_y, samples))


def solution(mesh):
    placed = (
        P("survey", "tile", None, None),
        P(None, "tile", None, None),
        P(None, "tile", None),
        P(),
    )
    return jax.shard_map(
        local,
        mesh=mesh,
        in_specs=placed,
        out_specs=(P("survey", None, "tile", None), P("survey", "tile", None, None)),
        check_vma=False,
    )
```

profile of v0, /device:TPU:0, one launch (start us, length us, event | category | flops | bytes accessed | tf_op | source)
XLA Modules:
  0.0 178.7 jit_solution(15932245381189353399)
XLA Ops:
  3.9 2.0 %gather_fusion.1 = bf16[512,256]{1,0:T(8,128)(2,1)S(1)} fusion(bf16[1024,256]{1,0:T(8,128)(2,1)S(1)} %multiply_convert_fusion.2, s32[1024]{0:T(1024)S(1)} %pad_clamp_fusion), kind=kCustom, calls=%fused_computation.1.clone | custom fusion | bytes 526336 | tf_op jit(solution)/shard_map/jit(_take)/gather | solution.py:68
  6.7 6.3 %all-to-all-start = ((bf16[4,128,256]{2,1,0:T(8,128)(2,1)}), bf16[4,128,256]{2,1,0:T(8,128)(2,1)S(1)}, u32[]{:S(2)}, u32[]{:S(2)}) async-start(bf16[4,128,256]{2,1,0:T(8,128)(2,1)} %broadcast_select_fusion.1), calls=%async_computation | async-start | bytes 524288 | tf_op jit(solution)/shard_map/all_to_all | solution.py:69
  13.8 2.0 %gather_fusion = bf16[512,256]{1,0:T(8,128)(2,1)S(1)} fusion(bf16[1024,256]{1,0:T(8,128)(2,1)S(1)} %multiply_convert_fusion.2, s32[1024]{0:T(1024)S(1)} %pad_clamp_fusion.1), kind=kCustom, calls=%fused_computation.clone | custom fusion | bytes 526336 | tf_op jit(solution)/shard_map/jit(_take)/gather | solution.py:107
  16.2 5.8 %all-to-all-done = bf16[4,128,256]{2,1,0:T(8,128)(2,1)S(1)} async-done(((bf16[4,128,256]{2,1,0:T(8,128)(2,1)}), bf16[4,128,256]{2,1,0:T(8,128)(2,1)S(1)}, u32[]{:S(2)}, u32[]{:S(2)}) %all-to-all-start) | async-done | bytes 262176 | tf_op jit(solution)/shard_map/all_to_all | solution.py:69
  23.6 2.4 %scatter_custom_fusion = f32[3,1024]{0,1:T(8,128)S(1)} fusion(s32[512]{0:T(512)S(1)} %fusion.66, f32[512,3]{1,0:T(8,128)S(1)} %bitcast.91, f32[]{:T(128)} %constant.66.clone.1), kind=kCustom, calls=%fused_computation.65 | custom fusion | flops 1536 | bytes 12292 | tf_op jit(solution)/shard_map/scatter-add | solution.py:110
  29.0 2.4 %scatter_custom_fusion.1 = f32[3,1024]{0,1:T(8,128)S(1)} fusion(s32[512]{0:T(512)S(1)} %fusion.66, f32[512,3]{1,0:T(8,128)S(1)} %bitcast.92, f32[]{:T(128)} %constant.76.clone.1), kind=kCustom, calls=%fused_computation.61 | custom fusion | flops 1536 | bytes 12292 | tf_op jit(solution)/shard_map/scatter-add | solution.py:111
  32.5 15.0 %all-reduce.14 = (f32[3]{0:T(128)S(1)}, f32[3]{0:T(128)S(1)}) all-reduce(f32[3]{0:T(128)S(1)} %multiply_reduce_fusion.3, f32[3]{0:T(128)S(1)} %get-tuple-element.51), channel_id=1, replica_groups=mesh['survey'=4,'tile'=8] {'tile'}, use_global_device_ids=true, to_apply=%region_8.10 | all-reduce | flops 6 | bytes 48 | tf_op jit(solution)/shard_map/psum | solution.py:80
  50.2 2.0 %collective-permute-done.2 = f32[3,1,128]{2,1,0:T(1,128)S(1)} collective-permute-done((f32[3,1,128]{2,1,0:T(1,128)S(1)}, f32[3,1,128]{2,1,0:T(1,128)S(1)}, u32[]{:S(2)}, u32[]{:S(2)}) %collective-permute-start.2) | collective-permute-done | bytes 1568 | tf_op jit(solution)/shard_map/ppermute | solution.py:22
  52.4 15.9 %all-reduce.13 = (f32[3]{0:T(128)S(1)}, f32[3]{0:T(128)S(1)}) all-reduce(f32[3]{0:T(128)S(1)} %get-tuple-element.26, f32[3]{0:T(128)S(1)} %get-tuple-element.25), channel_id=1, replica_groups=mesh['survey'=4,'tile'=8] {'tile'}, use_global_device_ids=true, to_apply=%region_15.17 | all-reduce | flops 6 | bytes 48 | tf_op jit(solution)/shard_map/psum | solution.py:80
  71.2 3.5 %collective-permute-done.4 = f32[3,1,128]{2,1,0:T(1,128)S(1)} collective-permute-done((f32[3,1,128]{2,1,0:T(1,128)S(1)}, f32[3,1,128]{2,1,0:T(1,128)S(1)}, u32[]{:S(2)}, u32[]{:S(2)}) %collective-permute-start.4) | collective-permute-done | bytes 1568 | tf_op jit(solution)/shard_map/ppermute | solution.py:22
  75.0 15.9 %all-reduce.12 = (f32[3]{0:T(128)S(1)}, f32[3]{0:T(128)S(1)}) all-reduce(f32[3]{0:T(128)S(1)} %get-tuple-element.24, f32[3]{0:T(128)S(1)} %get-tuple-element.23), channel_id=1, replica_groups=mesh['survey'=4,'tile'=8] {'tile'}, use_global_device_ids=true, to_apply=%region_19.21 | all-reduce | flops 6 | bytes 48 | tf_op jit(solution)/shard_map/psum | solution.py:80
  92.1 2.0 %gather_fusion.3 = bf16[512,256]{1,0:T(8,128)(2,1)S(1)} fusion(bf16[1024,256]{1,0:T(8,128)(2,1)S(1)} %multiply_convert_fusion.1, s32[1024]{0:T(1024)S(1)} %pad_clamp_fusion), kind=kCustom, calls=%fused_computation.3.clone | custom fusion | bytes 526336 | tf_op jit(solution)/shard_map/jit(_take)/gather | solution.py:68
  94.9 3.6 %all-to-all-start.1 = ((bf16[4,128,256]{2,1,0:T(8,128)(2,1)}), bf16[4,128,256]{2,1,0:T(8,128)(2,1)S(1)}, u32[]{:S(2)}, u32[]{:S(2)}) async-start(bf16[4,128,256]{2,1,0:T(8,128)(2,1)} %broadcast_select_fusion), calls=%async_computation.1 | async-start | bytes 524288 | tf_op jit(solution)/shard_map/all_to_all | solution.py:69
  98.5 2.0 %gather_fusion.2 = bf16[512,256]{1,0:T(8,128)(2,1)S(1)} fusion(bf16[1024,256]{1,0:T(8,128)(2,1)S(1)} %multiply_convert_fusion.1, s32[1024]{0:T(1024)S(1)} %pad_clamp_fusion.1), kind=kCustom, calls=%fused_computation.2.clone | custom fusion | bytes 526336 | tf_op jit(solution)/shard_map/jit(_take)/gather | solution.py:107
  100.6 6.5 %all-to-all-done.1 = bf16[4,128,256]{2,1,0:T(8,128)(2,1)S(1)} async-done(((bf16[4,128,256]{2,1,0:T(8,128)(2,1)}), bf16[4,128,256]{2,1,0:T(8,128)(2,1)S(1)}, u32[]{:S(2)}, u32[]{:S(2)}) %all-to-all-start.1) | async-done | bytes 262176 | tf_op jit(solution)/shard_map/all_to_all | solution.py:69
  108.7 2.4 %scatter_custom_fusion.2 = f32[3,1024]{0,1:T(8,128)S(1)} fusion(s32[512]{0:T(512)S(1)} %fusion.66, f32[512,3]{1,0:T(8,128)S(1)} %bitcast.90, f32[]{:T(128)} %constant.66.clone.1), kind=kCustom, calls=%fused_computation.63 | custom fusion | flops 1536 | bytes 12292 | tf_op jit(solution)/shard_map/scatter-add | solution.py:110
  114.2 2.4 %scatter_custom_fusion.3 = f32[3,1024]{0,1:T(8,128)S(1)} fusion(s32[512]{0:T(512)S(1)} %fusion.66, f32[512,3]{1,0:T(8,128)S(1)} %bitcast.89, f32[]{:T(128)} %constant.76.clone.1), kind=kCustom, calls=%fused_computation.59 | custom fusion | flops 1536 | bytes 12292 | tf_op jit(solution)/shard_map/scatter-add | solution.py:111
  116.8 2.2 %collective-permute-done.6 = f32[3,1,128]{2,1,0:T(1,128)S(1)} collective-permute-done((f32[3,1,128]{2,1,0:T(1,128)S(1)}, f32[3,1,128]{2,1,0:T(1,128)S(1)}, u32[]{:S(2)}, u32[]{:S(2)}) %collective-permute-start.6) | collective-permute-done | bytes 1568 | tf_op jit(solution)/shard_map/ppermute | solution.py:22
  119.3 14.1 %all-reduce.11 = (f32[3]{0:T(128)S(1)}, f32[3]{0:T(128)S(1)}) all-reduce(f32[3]{0:T(128)S(1)} %multiply_reduce_fusion.1, f32[3]{0:T(128)S(1)} %get-tuple-element.44), channel_id=1, replica_groups=mesh['survey'=4,'tile'=8] {'tile'}, use_global_device_ids=true, to_apply=%region_30.32 | all-reduce | flops 6 | bytes 48 | tf_op jit(solution)/shard_map/psum | solution.py:80
  136.1 2.1 %collective-permute-done.8 = f32[3,1,128]{2,1,0:T(1,128)S(1)} collective-permute-done((f32[3,1,128]{2,1,0:T(1,128)S(1)}, f32[3,1,128]{2,1,0:T(1,128)S(1)}, u32[]{:S(2)}, u32[]{:S(2)}) %collective-permute-start.8) | collective-permute-done | bytes 1568 | tf_op jit(solution)/shard_map/ppermute | solution.py:22
  138.5 15.7 %all-reduce.10 = (f32[3]{0:T(128)S(1)}, f32[3]{0:T(128)S(1)}) all-reduce(f32[3]{0:T(128)S(1)} %get-tuple-element.22, f32[3]{0:T(128)S(1)} %get-tuple-element.21), channel_id=1, replica_groups=mesh['survey'=4,'tile'=8] {'tile'}, use_global_device_ids=true, to_apply=%region_37.39 | all-reduce | flops 6 | bytes 48 | tf_op jit(solution)/shard_map/psum | solution.py:80
  157.0 3.5 %collective-permute-done.10 = f32[3,1,128]{2,1,0:T(1,128)S(1)} collective-permute-done((f32[3,1,128]{2,1,0:T(1,128)S(1)}, f32[3,1,128]{2,1,0:T(1,128)S(1)}, u32[]{:S(2)}, u32[]{:S(2)}) %collective-permute-start.10) | collective-permute-done | bytes 1568 | tf_op jit(solution)/shard_map/ppermute | solution.py:22
  160.8 15.9 %all-reduce.9 = (f32[3]{0:T(128)S(1)}, f32[3]{0:T(128)S(1)}) all-reduce(f32[3]{0:T(128)S(1)} %get-tuple-element.20, f32[3]{0:T(128)S(1)} %get-tuple-element.19), channel_id=1, replica_groups=mesh['survey'=4,'tile'=8] {'tile'}, use_global_device_ids=true, to_apply=%region_41.43 | all-reduce | flops 6 | bytes 48 | tf_op jit(solution)/shard_map/psum | solution.py:80
  176.8 1.9 %multiply_convert_fusion = bf16[1024,256]{1,0:T(8,128)(2,1)} fusion(bf16[1,8,128,256]{3,2,1,0:T(8,128)(2,1)S(1)} %copy-done.1, f32[1024]{0:T(1024)S(1)} %get-tuple-element.54, f32[1024]{0:T(1024)S(1)} %get-tuple-element.55, f32[1024]{0:T(1024)S(1)} %get-tuple-element.53, f32[256]{0:T(256)S(1)} %fusion.68, f32[1024,256]{1,0:T(8,128)S(1)} %bitcast_convert_fusion), kind=kLoop, calls=%fused_computation.11 | loop fusion | flops 2097152 | bytes 2110464 | tf_op jit(solution)/shard_map/convert_element_type | solution.py:40
  (102 shorter events, 30.2 us)
Async XLA Ops:
  0.6 15.2 %copy-start = (s32[4,1,4]{2,1,0:T(1,128)S(1)}, s32[4,1,4]{2,1,0:T(1,128)}, u32[]{:S(2)}) copy-start(s32[4,1,4]{2,1,0:T(1,128)} %param.8) | copy-start | bytes 196
  0.6 2.6 %copy-start.1 = (bf16[1,8,128,256]{3,2,1,0:T(8,128)(2,1)S(1)}, bf16[1,8,128,256]{3,2,1,0:T(8,128)(2,1)}, u32[]{:S(2)}) copy-start(bf16[1,8,128,256]{3,2,1,0:T(8,128)(2,1)} %param.6) | copy-start | bytes 1572868
  5.9 7.9 %copy-start.3 = (f32[3]{0:T(128)S(1)}, f32[3]{0:T(128)}, u32[]{:S(2)}) copy-start(f32[3]{0:T(128)} %param.9) | copy-start | bytes 40
  6.7 15.3 %all-to-all-start = ((bf16[4,128,256]{2,1,0:T(8,128)(2,1)}), bf16[4,128,256]{2,1,0:T(8,128)(2,1)S(1)}, u32[]{:S(2)}, u32[]{:S(2)}) async-start(bf16[4,128,256]{2,1,0:T(8,128)(2,1)} %broadcast_select_fusion.1), calls=%async_computation | async-start | bytes 524288 | tf_op jit(solution)/shard_map/all_to_all | solution.py:69
  26.1 5.5 %collective-permute-start.1 = (f32[3,1,128]{2,1,0:T(1,128)S(1)}, f32[3,1,128]{2,1,0:T(1,128)S(1)}, u32[]{:S(2)}, u32[]{:S(2)}) collective-permute-start(f32[3,1,128]{2,1,0:T(1,128)S(1)} %get-tuple-element.69), channel_id=1, source_target_pairs={{0,1},{1,2},{2,3},{3,4},{4,5},{5,6},{6,7},{8,9},{9,10},{10,11},{11... | collective-permute-start | bytes 4616 | tf_op jit(solution)/shard_map/ppermute | solution.py:21
  27.4 4.8 %collective-permute-start = (f32[3,1,128]{2,1,0:T(1,128)S(1)}, f32[3,1,128]{2,1,0:T(1,128)S(1)}, u32[]{:S(2)}, u32[]{:S(2)}) collective-permute-start(f32[3,1,128]{2,1,0:T(1,128)S(1)} %get-tuple-element.70), channel_id=1, source_target_pairs={{1,0},{2,1},{3,2},{4,3},{5,4},{6,5},{7,6},{9,8},{10,9},{11,10},{12... | collective-permute-start | bytes 4616 | tf_op jit(solution)/shard_map/ppermute | solution.py:22
  47.6 2.6 %collective-permute-start.3 = (f32[3,1,128]{2,1,0:T(1,128)S(1)}, f32[3,1,128]{2,1,0:T(1,128)S(1)}, u32[]{:S(2)}, u32[]{:S(2)}) collective-permute-start(f32[3,1,128]{2,1,0:T(1,128)S(1)} %get-tuple-element.67), channel_id=1, source_target_pairs={{0,1},{1,2},{2,3},{3,4},{4,5},{5,6},{6,7},{8,9},{9,10},{10,11},{11... | collective-permute-start | bytes 4616 | tf_op jit(solution)/shard_map/ppermute | solution.py:21
  48.9 3.3 %collective-permute-start.2 = (f32[3,1,128]{2,1,0:T(1,128)S(1)}, f32[3,1,128]{2,1,0:T(1,128)S(1)}, u32[]{:S(2)}, u32[]{:S(2)}) collective-permute-start(f32[3,1,128]{2,1,0:T(1,128)S(1)} %get-tuple-element.68), channel_id=1, source_target_pairs={{1,0},{2,1},{3,2},{4,3},{5,4},{6,5},{7,6},{9,8},{10,9},{11,10},{12... | collective-permute-start | bytes 4616 | tf_op jit(solution)/shard_map/ppermute | solution.py:22
  68.5 2.7 %collective-permute-start.5 = (f32[3,1,128]{2,1,0:T(1,128)S(1)}, f32[3,1,128]{2,1,0:T(1,128)S(1)}, u32[]{:S(2)}, u32[]{:S(2)}) collective-permute-start(f32[3,1,128]{2,1,0:T(1,128)S(1)} %get-tuple-element.65), channel_id=1, source_target_pairs={{0,1},{1,2},{2,3},{3,4},{4,5},{5,6},{6,7},{8,9},{9,10},{10,11},{11... | collective-permute-start | bytes 4616 | tf_op jit(solution)/shard_map/ppermute | solution.py:21
  69.9 4.8 %collective-permute-start.4 = (f32[3,1,128]{2,1,0:T(1,128)S(1)}, f32[3,1,128]{2,1,0:T(1,128)S(1)}, u32[]{:S(2)}, u32[]{:S(2)}) collective-permute-start(f32[3,1,128]{2,1,0:T(1,128)S(1)} %get-tuple-element.66), channel_id=1, source_target_pairs={{1,0},{2,1},{3,2},{4,3},{5,4},{6,5},{7,6},{9,8},{10,9},{11,10},{12... | collective-permute-start | bytes 4616 | tf_op jit(solution)/shard_map/ppermute | solution.py:22
  94.9 12.2 %all-to-all-start.1 = ((bf16[4,128,256]{2,1,0:T(8,128)(2,1)}), bf16[4,128,256]{2,1,0:T(8,128)(2,1)S(1)}, u32[]{:S(2)}, u32[]{:S(2)}) async-start(bf16[4,128,256]{2,1,0:T(8,128)(2,1)} %broadcast_select_fusion), calls=%async_computation.1 | async-start | bytes 524288 | tf_op jit(solution)/shard_map/all_to_all | solution.py:69
  111.3 5.5 %collective-permute-start.7 = (f32[3,1,128]{2,1,0:T(1,128)S(1)}, f32[3,1,128]{2,1,0:T(1,128)S(1)}, u32[]{:S(2)}, u32[]{:S(2)}) collective-permute-start(f32[3,1,128]{2,1,0:T(1,128)S(1)} %get-tuple-element.60), channel_id=1, source_target_pairs={{0,1},{1,2},{2,3},{3,4},{4,5},{5,6},{6,7},{8,9},{9,10},{10,11},{11... | collective-permute-start | bytes 4616 | tf_op jit(solution)/shard_map/ppermute | solution.py:21
  112.6 6.4 %collective-permute-start.6 = (f32[3,1,128]{2,1,0:T(1,128)S(1)}, f32[3,1,128]{2,1,0:T(1,128)S(1)}, u32[]{:S(2)}, u32[]{:S(2)}) collective-permute-start(f32[3,1,128]{2,1,0:T(1,128)S(1)} %get-tuple-element.61), channel_id=1, source_target_pairs={{1,0},{2,1},{3,2},{4,3},{5,4},{6,5},{7,6},{9,8},{10,9},{11,10},{12... | collective-permute-start | bytes 4616 | tf_op jit(solution)/shard_map/ppermute | solution.py:22
  133.5 2.6 %collective-permute-start.9 = (f32[3,1,128]{2,1,0:T(1,128)S(1)}, f32[3,1,128]{2,1,0:T(1,128)S(1)}, u32[]{:S(2)}, u32[]{:S(2)}) collective-permute-start(f32[3,1,128]{2,1,0:T(1,128)S(1)} %get-tuple-element.58), channel_id=1, source_target_pairs={{0,1},{1,2},{2,3},{3,4},{4,5},{5,6},{6,7},{8,9},{9,10},{10,11},{11... | collective-permute-start | bytes 4616 | tf_op jit(solution)/shard_map/ppermute | solution.py:21
  134.8 3.4 %collective-permute-start.8 = (f32[3,1,128]{2,1,0:T(1,128)S(1)}, f32[3,1,128]{2,1,0:T(1,128)S(1)}, u32[]{:S(2)}, u32[]{:S(2)}) collective-permute-start(f32[3,1,128]{2,1,0:T(1,128)S(1)} %get-tuple-element.59), channel_id=1, source_target_pairs={{1,0},{2,1},{3,2},{4,3},{5,4},{6,5},{7,6},{9,8},{10,9},{11,10},{12... | collective-permute-start | bytes 4616 | tf_op jit(solution)/shard_map/ppermute | solution.py:22
  154.3 2.7 %collective-permute-start.11 = (f32[3,1,128]{2,1,0:T(1,128)S(1)}, f32[3,1,128]{2,1,0:T(1,128)S(1)}, u32[]{:S(2)}, u32[]{:S(2)}) collective-permute-start(f32[3,1,128]{2,1,0:T(1,128)S(1)} %get-tuple-element.56), channel_id=1, source_target_pairs={{0,1},{1,2},{2,3},{3,4},{4,5},{5,6},{6,7},{8,9},{9,10},{10,11},{11... | collective-permute-start | bytes 4616 | tf_op jit(solution)/shard_map/ppermute | solution.py:21
  155.7 4.8 %collective-permute-start.10 = (f32[3,1,128]{2,1,0:T(1,128)S(1)}, f32[3,1,128]{2,1,0:T(1,128)S(1)}, u32[]{:S(2)}, u32[]{:S(2)}) collective-permute-start(f32[3,1,128]{2,1,0:T(1,128)S(1)} %get-tuple-element.57), channel_id=1, source_target_pairs={{1,0},{2,1},{3,2},{4,3},{5,4},{6,5},{7,6},{9,8},{10,9},{11,10},{12... | collective-permute-start | bytes 4616 | tf_op jit(solution)/shard_map/ppermute | solution.py:22
  176.8 1.9 %copy-start.2 = (f32[3,8,128]{2,1,0:T(8,128)}, f32[3,8,128]{2,1,0:T(8,128)S(1)}, u32[]{:S(2)}) copy-start(f32[3,8,128]{2,1,0:T(8,128)S(1)} %add_add_fusion) | copy-start | bytes 36868
where the time goes:
time: 181 us; the launch traced here: 179 us
  blocking collectives  92.5 us (51%)
  waiting for transfers between devices  26.3 us (15%)
  starting transfers between devices  25.6 us (14%)
  other arithmetic  23 us (13%)
  local copies, waits for them, and re-layouts  10.1 us (6%)
    psum x6, blocking collectives, paired(): lax.psum((jnp.sum(residual * residual, axis=(1, 2)), jnp.sum(residual * i...  92.5 us
    ppermute x6, waiting for transfers between devices, extended(): after = lax.ppermute(leading, axis, down)  14 us
    all_to_all x2, waiting for transfers between devices, send_traces(): lax.all_to_all(outgoing, 'survey', split_axis=0, concat_axis=0, tiled=True)  12.3 us
    all_to_all x2, starting transfers between devices, send_traces(): lax.all_to_all(outgoing, 'survey', split_axis=0, concat_axis=0, tiled=True)  9.93 us
    ppermute x6, starting transfers between devices, extended(): before = lax.ppermute(last, axis, up)  7.95 us
    ppermute x6, starting transfers between devices, extended(): after = lax.ppermute(leading, axis, down)  7.75 us
    scatter-add x2, other arithmetic, solve_round(): empty_sum.at[:, recv_index].add(numerator).reshape(3, rows_x, rows_y)  4.76 us
    scatter-add x2, other arithmetic, solve_round(): empty_sum.at[:, recv_index].add(denominator).reshape(3, rows_x, rows_y)  4.76 us
  transfers between devices with their start and end apart: 14, of which 8 were waited for; matrix products, arithmetic and copies ran while one was open for 6% of the time, Pallas kernels for 0%

commit v1 on v0

v1 whole, which is shorter than its diff:
```python
import functools

import jax
import jax.numpy as jnp
from jax import lax
from jax.experimental import pallas as pl
from jax.experimental.pallas import tpu as pltpu
from jax.sharding import PartitionSpec as P

ROUNDS = 2
CG_ITERS = 3

damping = 0.05
sim_eps = 1e-05

f32 = jnp.float32
VMEM = pl.BlockSpec(memory_space=pltpu.VMEM)
SMEM = pl.BlockSpec(memory_space=pltpu.SMEM)
PARAMS = pltpu.CompilerParams(vmem_limit_bytes=16 * 1024 * 1024)


def partner_of(me, k, n):
    if n & (n - 1) == 0:
        return me ^ k
    return lax.rem(me + k, n)


def sender_to(me, k, n):
    if n & (n - 1) == 0:
        return me ^ k
    return lax.rem(me + n - k, n)


def shift_pairs(k, n):
    if n & (n - 1) == 0:
        return [(i, i ^ k) for i in range(n)]
    return [(i, (i + k) % n) for i in range(n)]


def time_row(samples):
    i = lax.broadcasted_iota(jnp.int32, (1, samples), 1).astype(f32)
    return (i - (samples - 1) / 2.0) / (samples / 2.0)


def slope_matrix(samples):
    row = lax.broadcasted_iota(jnp.int32, (samples, samples), 0)
    col = lax.broadcasted_iota(jnp.int32, (samples, samples), 1)
    up = jnp.where(row == col + 1, 0.5, 0.0)
    down = jnp.where(row == col - 1, 0.5, 0.0)
    return (up - down).astype(jnp.bfloat16)


def eye_mask(rows, lanes):
    row = lax.broadcasted_iota(jnp.int32, (rows, lanes), 0)
    col = lax.broadcasted_iota(jnp.int32, (rows, lanes), 1)
    return row == col


def to_lanes(column, eye):
    return jnp.sum(jnp.where(eye, column, 0.0), axis=0, keepdims=True)


def to_column(row, eye):
    return jnp.sum(jnp.where(eye, row, 0.0), axis=1, keepdims=True)


def window_of(start, total, cap):
    base = jnp.minimum((start // 8) * 8, total - cap - 8)
    return pl.multiple_of(base, 8), start - base


def corrected_rows(raw, shift, gain, trend, slope_mat, time_pos):
    slope = jnp.dot(raw, slope_mat, preferred_element_type=f32)
    amplitude = jnp.exp(gain + trend * time_pos)
    return (amplitude * (raw.astype(f32) + shift * slope)).astype(jnp.bfloat16)


def pack_kernel(n, index_ref, data_ref, *out_refs):
    me = lax.axis_index("survey")
    total, cap = data_ref.shape[0], out_refs[0].shape[0]
    sub = lax.broadcasted_iota(jnp.int32, (8, data_ref.shape[1]), 0)
    for k in range(1, n):
        base, off = window_of(index_ref[me, partner_of(me, k, n)], total, cap)
        out = out_refs[k - 1]
        out[8:, :] = data_ref[pl.ds(base + 8, cap - 8), :]
        first = data_ref[pl.ds(base, 8), :].astype(f32)
        last = data_ref[pl.ds(base + cap, 8), :].astype(f32)
        out[:8, :] = jnp.where(sub >= off, first, last).astype(out.dtype)


def energies(rows, slope_mat, time_pos, eye, scale):
    vals = rows.astype(f32)
    moved = jnp.dot(rows, slope_mat, preferred_element_type=f32)
    tilted = time_pos * vals
    return [
        to_lanes(jnp.sum(part * part, axis=1, keepdims=True) * scale, eye)
        for part in (moved, vals, tilted)
    ]


def own_first_kernel(data_ref, energy_ref):
    rows_x, rows_y = energy_ref.shape[1:]
    samples = data_ref.shape[1]
    slope_mat, time_pos = slope_matrix(samples), time_row(samples)
    eye = eye_mask(rows_y, rows_y)
    for x in range(rows_x):
        rows = data_ref[x * rows_y : (x + 1) * rows_y, :]
        for c, row in enumerate(energies(rows, slope_mat, time_pos, eye, 1.0 / samples)):
            energy_ref[c, x : x + 1, :] = row


def own_next_kernel(data_ref, fields_ref, current_ref, energy_ref):
    rows_x, rows_y = energy_ref.shape[1:]
    samples = data_ref.shape[1]
    slope_mat, time_pos = slope_matrix(samples), time_row(samples)
    eye = eye_mask(rows_y, rows_y)
    for x in range(rows_x):
        block = slice(x * rows_y, (x + 1) * rows_y)
        columns = [to_column(fields_ref[c, x : x + 1, :], eye) for c in range(3)]
        rows = corrected_rows(data_ref[block, :], *columns, slope_mat, time_pos)
        current_ref[block, :] = rows
        for c, row in enumerate(energies(rows, slope_mat, time_pos, eye, 1.0 / samples)):
            energy_ref[c, x : x + 1, :] = row


def pair_kernel(n, second, index_ref, count_ref, own_ref, energy_ref, *refs):
    partner_refs = refs[: n - 1]
    field_refs = refs[n - 1 : 2 * (n - 1)] if second else None
    out_ref = refs[-1]
    me = lax.axis_index("survey")
    total, samples = own_ref.shape
    cap = partner_refs[0].shape[0]
    rows_x, rows_y = energy_ref.shape[1:]
    scale = 1.0 / samples
    slope_mat, time_pos = slope_matrix(samples), time_row(samples)
    eye, eye8 = eye_mask(cap, rows_y), eye_mask(8, rows_y)
    grid_x = lax.broadcasted_iota(jnp.int32, (rows_x, rows_y), 0)
    grid_y = lax.broadcasted_iota(jnp.int32, (rows_x, rows_y), 1)
    position = grid_x * rows_y + grid_y
    energy = energy_ref[1]
    target = [jnp.zeros((rows_x, rows_y), f32) for _ in range(3)]
    similar = jnp.zeros((rows_x, rows_y), f32)
    for k in range(1, n):
        source = sender_to(me, k, n)
        start, count = index_ref[source, me], count_ref[source, me]
        base, off = window_of(start, total, cap)
        first_x = base // rows_y
        first_y = base - first_x * rows_y
        raw = partner_refs[k - 1][...]
        if second:
            lane = lax.broadcasted_iota(jnp.int32, (1, rows_y), 1)
            columns = []
            for c in range(3):
                here = field_refs[k - 1][c, pl.ds(first_x, 1), :]
                after = field_refs[k - 1][c, pl.ds(first_x + 1, 1), :]
                wrapped = jnp.where(lane >= first_y + off, here, after)
                wide = jnp.broadcast_to(wrapped, (8, rows_y))
                wide = pltpu.roll(wide, lax.rem(rows_y - first_y, rows_y), 1)
                columns.append(to_column(wide[:1], eye))
            raw = corrected_rows(raw, *columns, slope_mat, time_pos)
        partner = raw.astype(f32)
        own_rows = own_ref[pl.ds(base, cap + 8), :]
        moved = jnp.dot(own_rows, slope_mat, preferred_element_type=f32)
        own = own_rows.astype(f32)

        def reduced(part_own, part_moved, part_partner, mask):
            residual = part_partner - part_own
            along = residual * part_own
            parts = (
                residual * part_moved,
                along,
                residual * (time_pos * part_own),
                part_own * part_partner,
                part_partner * part_partner,
            )
            return [to_lanes(jnp.sum(q, axis=1, keepdims=True) * scale, mask) for q in parts]

        main = reduced(own[:cap], moved[:cap], partner, eye)
        tail = reduced(own[cap:], moved[cap:], partner[:8], eye8)
        chosen = (grid_x == first_x) | (grid_y < first_y)
        placed = []
        for q in range(5):
            a = pltpu.roll(jnp.broadcast_to(main[q], (rows_x, rows_y)), first_y, 1)
            b = pltpu.roll(jnp.broadcast_to(tail[q], (rows_x, rows_y)), first_y, 1)
            placed.append(jnp.where(chosen, a, b))
        cross_term, other_energy = placed[3], placed[4]
        live = (position >= start) & (position < start + count)
        weight = cross_term * cross_term / ((energy + sim_eps) * (other_energy + sim_eps))
        weight = jnp.where(live, weight, 0.0)
        similar = similar + weight
        for c in range(3):
            target[c] = target[c] + weight * placed[c]
    for c in range(3):
        out_ref[c] = target[c]
        out_ref[3 + c] = similar * energy_ref[c]


def grid_solve(masks, smoothing_ref, piece_refs, grid_ref, tile):
    rows_x = piece_refs[0].shape[1]
    for piece, mask in zip(piece_refs, masks):
        spot = pl.multiple_of((tile ^ mask) * rows_x, rows_x)
        for c in range(6):
            grid_ref[c, pl.ds(spot, rows_x), :] = piece[c]
    size_x, size_y = grid_ref.shape[1:]
    grid_x = lax.broadcasted_iota(jnp.int32, (size_x, size_y), 0)
    grid_y = lax.broadcasted_iota(jnp.int32, (size_x, size_y), 1)

    def total(q):
        return jnp.sum(q, keepdims=True)

    def beside(v):
        return (
            jnp.where(grid_x > 0, pltpu.roll(v, 1, 0), 0.0)
            + jnp.where(grid_x < size_x - 1, pltpu.roll(v, size_x - 1, 0), 0.0)
            + jnp.where(grid_y > 0, pltpu.roll(v, 1, 1), 0.0)
            + jnp.where(grid_y < size_y - 1, pltpu.roll(v, size_y - 1, 1), 0.0)
        )

    updates = []
    for c in range(3):
        strength = smoothing_ref[c]
        diagonal = grid_ref[3 + c] + (damping + 4.0 * strength)
        residual = grid_ref[c]
        direction = residual
        norm_now = total(residual * residual)
        update = None
        for iteration in range(CG_ITERS):
            image = diagonal * direction - strength * beside(direction)
            alpha = norm_now / total(direction * image)
            step = alpha * direction
            update = step if update is None else update + step
            if iteration + 1 < CG_ITERS:
                residual = residual - alpha * image
                norm_next = total(residual * residual)
                direction = residual + (norm_next / norm_now) * direction
                norm_now = norm_next
        updates.append(update)
    return updates


def solve_first_kernel(masks, smoothing_ref, *refs):
    pieces, fields_ref, grid_ref = refs[: len(masks)], refs[-2], refs[-1]
    tile = lax.axis_index("tile")
    updates = grid_solve(masks, smoothing_ref, pieces, grid_ref, tile)
    rows_x = fields_ref.shape[1]
    for c in range(3):
        grid_ref[c] = updates[c]
        fields_ref[c] = grid_ref[c, pl.ds(pl.multiple_of(tile * rows_x, rows_x), rows_x), :]


def solve_last_kernel(masks, smoothing_ref, before_ref, data_ref, *refs):
    pieces, fields_ref, volume_ref, grid_ref = refs[: len(masks)], refs[-3], refs[-2], refs[-1]
    tile = lax.axis_index("tile")
    updates = grid_solve(masks, smoothing_ref, pieces, grid_ref, tile)
    rows_x, rows_y = fields_ref.shape[1:]
    for c in range(3):
        grid_ref[c] = updates[c]
        mine = grid_ref[c, pl.ds(pl.multiple_of(tile * rows_x, rows_x), rows_x), :]
        fields_ref[c] = before_ref[c] + mine
    samples = data_ref.shape[1]
    slope_mat, time_pos = slope_matrix(samples), time_row(samples)
    eye = eye_mask(rows_y, rows_y)
    for x in range(rows_x):
        block = slice(x * rows_y, (x + 1) * rows_y)
        columns = [to_column(fields_ref[c, x : x + 1, :], eye) for c in range(3)]
        volume_ref[block, :] = corrected_rows(data_ref[block, :], *columns, slope_mat, time_pos)


def gather_tiles(piece, n):
    pieces = {0: piece}
    for mask in range(2, n, 2):
        pieces[mask] = lax.ppermute(piece, "tile", [(i, i ^ mask) for i in range(n)])
    if n > 1:
        for mask in list(pieces):
            pieces[mask + 1] = lax.ppermute(pieces[mask], "tile", [(i, i ^ 1) for i in range(n)])
    masks = sorted(pieces)
    return masks, [pieces[m] for m in masks]


def exchange(arrays, n):
    return [lax.ppermute(a, "survey", shift_pairs(k, n)) for k, a in zip(range(1, n), arrays)]


def local(n_survey, n_tile, data, correlation_index, correlation_count, smoothing):
    rows_x, rows_y, samples = data.shape[1:]
    total, cap = rows_x * rows_y, correlation_index.shape[-1]
    raw = data.reshape(total, samples)
    starts = correlation_index[:, 0, :, 0]
    counts = correlation_count[:, 0, :]
    packed = jax.ShapeDtypeStruct((cap, samples), data.dtype)
    field_shape = jax.ShapeDtypeStruct((3, rows_x, rows_y), f32)
    term_shape = jax.ShapeDtypeStruct((6, rows_x, rows_y), f32)
    raw_shape = jax.ShapeDtypeStruct((total, samples), data.dtype)
    grid = pltpu.VMEM((6, rows_x * n_tile, rows_y), f32)

    outgoing = pl.pallas_call(
        functools.partial(pack_kernel, n_survey),
        out_shape=[packed] * (n_survey - 1),
        in_specs=[SMEM, VMEM],
        out_specs=[VMEM] * (n_survey - 1),
        compiler_params=PARAMS,
        name="pack",
    )(starts, raw)
    arrived = exchange(outgoing, n_survey)
    energy = pl.pallas_call(
        own_first_kernel, out_shape=field_shape, in_specs=[VMEM], out_specs=VMEM, compiler_params=PARAMS, name="own_first"
    )(raw)
    terms = pl.pallas_call(
        functools.partial(pair_kernel, n_survey, False),
        out_shape=term_shape,
        in_specs=[SMEM] * 2 + [VMEM] * (n_survey + 1),
        out_specs=VMEM,
        compiler_params=PARAMS,
        name="pair_first",
    )(starts, counts, raw, energy, *arrived)
    masks, pieces = gather_tiles(terms, n_tile)
    fields = pl.pallas_call(
        functools.partial(solve_first_kernel, masks),
        out_shape=field_shape,
        in_specs=[SMEM] + [VMEM] * n_tile,
        out_specs=VMEM,
        scratch_shapes=[grid],
        compiler_params=PARAMS,
        name="solve_first",
    )(smoothing, *pieces)

    partner_fields = exchange([fields] * (n_survey - 1), n_survey)
    current, energy = pl.pallas_call(
        own_next_kernel,
        out_shape=[raw_shape, field_shape],
        in_specs=[VMEM] * 2,
        out_specs=[VMEM] * 2,
        compiler_params=PARAMS,
        name="own_next",
    )(raw, fields)
    terms = pl.pallas_call(
        functools.partial(pair_kernel, n_survey, True),
        out_shape=term_shape,
        in_specs=[SMEM] * 2 + [VMEM] * (2 * n_survey),
        out_specs=VMEM,
        compiler_params=PARAMS,
        name="pair_next",
    )(starts, counts, current, energy, *arrived, *partner_fields)
    masks, pieces = gather_tiles(terms, n_tile)
    fields, volume = pl.pallas_call(
        functools.partial(solve_last_kernel, masks),
        out_shape=[field_shape, raw_shape],
        in_specs=[SMEM] + [VMEM] * (n_tile + 2),
        out_specs=[VMEM] * 2,
        scratch_shapes=[grid],
        compiler_params=PARAMS,
        name="solve_last",
    )(smoothing, fields, raw, *pieces)
    return fields.reshape(1, 3, rows_x, rows_y), volume.reshape(1, rows_x, rows_y, samples)


def solution(mesh):
    placed = (
        P("survey", "tile", None, None),
        P(None, "tile", None, None),
        P(None, "tile", None),
        P(),
    )
    return jax.shard_map(
        functools.partial(local, mesh.shape["survey"], mesh.shape["tile"]),
        mesh=mesh,
        in_specs=placed,
        out_specs=(P("survey", None, "tile", None), P("survey", "tile", None, None)),
        check_vma=False,
    )
```

time: 181 us -> 46.8 us (0.26); the launches traced: 179 us -> 46.6 us
  blocking collectives: 92.5 us -> 0 us
  other arithmetic: 23 us -> 0 us
  Pallas kernels: 0 us -> 12.7 us
  waiting for transfers between devices: 26.3 us -> 14 us
  starting transfers between devices: 25.6 us -> 17.3 us
  local copies, waits for them, and re-layouts: 10.1 us -> 1.89 us
    psum x6 -> x0, blocking collectives: 92.5 us -> none  [paired(): lax.psum((jnp.sum(residual * residual, axis=(1, 2)), jnp.sum(residual * i...]
    pallas_call x0 -> x7, Pallas kernels: none -> 12.7 us  [the longest x1 4 us: local(): pl.pallas_call(functools.partial(solve_last_kernel, masks), out_shape=[fi...]
    all_to_all x2 -> x0, waiting for transfers between devices: 12.3 us -> none  [send_traces(): lax.all_to_all(outgoing, 'survey', split_axis=0, concat_axis=0, tiled=True)]
    all_to_all x2 -> x0, starting transfers between devices: 9.93 us -> none  [send_traces(): lax.all_to_all(outgoing, 'survey', split_axis=0, concat_axis=0, tiled=True)]
    scatter-add x4 -> x0, other arithmetic: 9.52 us -> none  [the longest x2 4.76 us: solve_round(): empty_sum.at[:, recv_index].add(numerator).reshape(3, rows_x, rows_y)]
    gather x4 -> x0, local copies, waits for them, and re-layouts: 7.81 us -> none  [the longest x2 3.91 us: send_traces(): outgoing = jnp.take(current, send_index, axis=0)]
    convert_element_type x6 -> x0, other arithmetic: 4.99 us -> none  [the longest x3 3.59 us: corrected(): (amplitude * (values + time_shift[..., None] * time_slope(values))).astyp...]
    reduce_sum x10 -> x0, other arithmetic: 3.98 us -> none  [the longest x2 2.61 us: pair_terms(): cross_term = jnp.mean(own_vals * partner_vals, axis=-1)]
  transfers between devices with their start and end apart: 14 -> 20, of which waited for: 8 -> 14; matrix products, arithmetic and copies ran while one was open for 6% -> 0% of each run, Pallas kernels for 0% -> 4%
where the time goes in v1:
time: 46.8 us; the launch traced here: 46.6 us
  starting transfers between devices  17.3 us (37%)
  waiting for transfers between devices  14 us (30%)
  Pallas kernels  12.7 us (27%)
  local copies, waits for them, and re-layouts  1.89 us (4%)
  between operations  0.73 us (2%)
    ppermute x6, starting transfers between devices, exchange(): lax.ppermute(a, 'survey', shift_pairs(k, n))  10.2 us
    ppermute x6, starting transfers between devices, gather_tiles(): lax.ppermute(piece, 'tile', [(i, i ^ mask) for i in range(n)])  7.11 us
    ppermute x6, waiting for transfers between devices, exchange(): lax.ppermute(a, 'survey', shift_pairs(k, n))  6.01 us
    ppermute x6, waiting for transfers between devices, gather_tiles(): lax.ppermute(piece, 'tile', [(i, i ^ mask) for i in range(n)])  5.61 us
    pallas_call x1, Pallas kernels, local(): pl.pallas_call(functools.partial(solve_last_kernel, masks), out_shape=[fi...  4 us
    pallas_call x1, Pallas kernels, local(): pl.pallas_call(functools.partial(solve_first_kernel, masks), out_shape=fi...  2.82 us
    ppermute x8, waiting for transfers between devices, gather_tiles(): lax.ppermute(pieces[mask], 'tile', [(i, i ^ 1) for i in range(n)])  2.37 us
    pallas_call x1, Pallas kernels, local(): pl.pallas_call(functools.partial(pair_kernel, n_survey, True), out_shape=...  1.93 us
  transfers between devices with their start and end apart: 20, of which 14 were waited for; matrix products, arithmetic and copies ran while one was open for 0% of the time, Pallas kernels for 4%

profile of v1, /device:TPU:0, one launch (start us, length us, event | category | flops | bytes accessed | tf_op | source)
XLA Modules:
  0.0 46.6 jit_solution(168448938206724803)
XLA Ops:
  0.6 0.8 %slice_reduce_fusion.index_ref = s32[4,4]{1,0:T(4,128)S(1)} fusion(s32[4,1,4,128]{3,2,1,0:T(4,128)} %param.5), kind=kLoop, calls=%fused_computation | loop fusion | bytes 128 | tf_op jit(solution)/shard_map/slice | solution.py:288
  1.5 1.0 %copy-done = bf16[1,8,128,256]{3,2,1,0:T(8,128)(2,1)S(1)} copy-done((bf16[1,8,128,256]{3,2,1,0:T(8,128)(2,1)S(1)}, bf16[1,8,128,256]{3,2,1,0:T(8,128)(2,1)}, u32[]{:S(2)}) %copy-start) | copy-done | bytes 524312
  2.5 0.6 %pack.1 = (bf16[128,256]{1,0:T(8,128)(2,1)S(1)}, bf16[128,256]{1,0:T(8,128)(2,1)S(1)}, bf16[128,256]{1,0:T(8,128)(2,1)S(1)}) custom-call(s32[4,4]{1,0:T(4,128)S(1)} %slice_reduce_fusion.index_ref, bf16[1024,256]{1,0:T(8,128)(2,1)S(1)} %bitcast.4), custom_call_target="tpu_custom_call" | custom-call | tf_op jit(solution)/shard_map/pack/pallas_call | solution.py:296
  3.1 3.1 %collective-permute-start = (bf16[128,256]{1,0:T(8,128)(2,1)S(1)}, bf16[128,256]{1,0:T(8,128)(2,1)S(1)}, u32[]{:S(2)}, u32[]{:S(2)}) collective-permute-start(bf16[128,256]{1,0:T(8,128)(2,1)S(1)} %get-tuple-element.9), channel_id=1, source_target_pairs={{0,8},{8,0},{16,24},{24,16},{1,9},{9,1},{17,25},{25,17},{2,10},{10... | collective-permute-start | bytes 196616 | tf_op jit(solution)/shard_map/ppermute | solution.py:281
  6.3 2.6 %collective-permute-start.1 = (bf16[128,256]{1,0:T(8,128)(2,1)S(1)}, bf16[128,256]{1,0:T(8,128)(2,1)S(1)}, u32[]{:S(2)}, u32[]{:S(2)}) collective-permute-start(bf16[128,256]{1,0:T(8,128)(2,1)S(1)} %get-tuple-element.10), channel_id=1, source_target_pairs={{0,16},{8,24},{16,0},{24,8},{1,17},{9,25},{17,1},{25,9},{2,18},{10... | collective-permute-start | bytes 196616 | tf_op jit(solution)/shard_map/ppermute | solution.py:281
  8.9 0.6 %own_first.1.energy_ref = f32[3,8,128]{2,1,0:T(8,128)S(1)} custom-call(bf16[1024,256]{1,0:T(8,128)(2,1)S(1)} %bitcast.5), custom_call_target="tpu_custom_call" | custom-call | tf_op jit(solution)/shard_map/own_first/pallas_call | solution.py:305
  9.4 4.1 %collective-permute-done.1.refs_1_ = bf16[128,256]{1,0:T(8,128)(2,1)S(1)} collective-permute-done((bf16[128,256]{1,0:T(8,128)(2,1)S(1)}, bf16[128,256]{1,0:T(8,128)(2,1)S(1)}, u32[]{:S(2)}, u32[]{:S(2)}) %collective-permute-start.1) | collective-permute-done | bytes 65568 | tf_op jit(solution)/shard_map/ppermute | solution.py:281
  13.5 1.4 %collective-permute-done.2.refs_2_ = bf16[128,256]{1,0:T(8,128)(2,1)S(1)} collective-permute-done((bf16[128,256]{1,0:T(8,128)(2,1)S(1)}, bf16[128,256]{1,0:T(8,128)(2,1)S(1)}, u32[]{:S(2)}, u32[]{:S(2)}) %collective-permute-start.2) | collective-permute-done | bytes 65568 | tf_op jit(solution)/shard_map/ppermute | solution.py:281
  14.9 1.3 %pair_first.1.refs_0_ = f32[6,8,128]{2,1,0:T(8,128)S(1)} custom-call(s32[4,4]{1,0:T(4,128)S(1)} %slice_reduce_fusion.index_ref, s32[4,4]{1,0:T(4,128)S(1)} %bitcast.9, bf16[1024,256]{1,0:T(8,128)(2,1)S(1)} %bitcast.6, f32[3,8,128]{2,1,0:T(8,128)S(1)} %own_first.1.energy_ref, bf16[128,256]{1,0:T(8,128)(2,1)S(1)} %collective-permute-done.refs_0_, ...), custom_call_target="tpu_custom_call" | custom-call | tf_op jit(solution)/shard_map/pair_first/pallas_call | solution.py:308
  16.2 2.5 %collective-permute-start.8 = (f32[6,8,128]{2,1,0:T(8,128)S(1)}, f32[6,8,128]{2,1,0:T(8,128)S(1)}, u32[]{:S(2)}, u32[]{:S(2)}) collective-permute-start(f32[6,8,128]{2,1,0:T(8,128)S(1)} %pair_first.1.refs_0_), channel_id=1, source_target_pairs={{0,6},{1,7},{2,4},{3,5},{4,2},{5,3},{6,0},{7,1},{8,14},{9,15},{10,... | collective-permute-start | bytes 73736 | tf_op jit(solution)/shard_map/ppermute | solution.py:272
  19.8 1.2 %collective-permute-done.8.refs_6_ = f32[6,8,128]{2,1,0:T(8,128)S(1)} collective-permute-done((f32[6,8,128]{2,1,0:T(8,128)S(1)}, f32[6,8,128]{2,1,0:T(8,128)S(1)}, u32[]{:S(2)}, u32[]{:S(2)}) %collective-permute-start.8) | collective-permute-done | bytes 24608 | tf_op jit(solution)/shard_map/ppermute | solution.py:272
  21.0 1.5 %collective-permute-done.6.refs_4_ = f32[6,8,128]{2,1,0:T(8,128)S(1)} collective-permute-done((f32[6,8,128]{2,1,0:T(8,128)S(1)}, f32[6,8,128]{2,1,0:T(8,128)S(1)}, u32[]{:S(2)}, u32[]{:S(2)}) %collective-permute-start.6) | collective-permute-done | bytes 24608 | tf_op jit(solution)/shard_map/ppermute | solution.py:272
  23.1 0.7 %collective-permute-done.7.refs_5_ = f32[6,8,128]{2,1,0:T(8,128)S(1)} collective-permute-done((f32[6,8,128]{2,1,0:T(8,128)S(1)}, f32[6,8,128]{2,1,0:T(8,128)S(1)}, u32[]{:S(2)}, u32[]{:S(2)}) %collective-permute-start.7) | collective-permute-done | bytes 24608 | tf_op jit(solution)/shard_map/ppermute | solution.py:275
  24.3 2.8 %solve_first.1.fields_ref.before_ref = f32[3,8,128]{2,1,0:T(8,128)S(1)} custom-call(f32[3]{0:T(128)S(1)} %copy-done.3, f32[6,8,128]{2,1,0:T(8,128)S(1)} %pair_first.1.refs_0_, f32[6,8,128]{2,1,0:T(8,128)S(1)} %collective-permute-done.3.refs_1_, f32[6,8,128]{2,1,0:T(8,128)S(1)} %collective-permute-done.4.refs_2_, ...), custom_call_target="tpu_custom_call" | custom-call | tf_op jit(solution)/shard_map/solve_first/pallas_call | solution.py:317
  27.1 1.8 %collective-permute-start.12 = (f32[3,8,128]{2,1,0:T(8,128)S(1)}, f32[3,8,128]{2,1,0:T(8,128)S(1)}, u32[]{:S(2)}, u32[]{:S(2)}) collective-permute-start(f32[3,8,128]{2,1,0:T(8,128)S(1)} %solve_first.1.fields_ref.before_ref), channel_id=1, source_target_pairs={{0,24},{8,16},{16,8},{24,0},{1,25},{9,17},{17,9},{25,1},{2,26},{10... | collective-permute-start | bytes 36872 | tf_op jit(solution)/shard_map/ppermute | solution.py:281
  29.0 2.6 %collective-permute-start.10 = (f32[3,8,128]{2,1,0:T(8,128)S(1)}, f32[3,8,128]{2,1,0:T(8,128)S(1)}, u32[]{:S(2)}, u32[]{:S(2)}) collective-permute-start(f32[3,8,128]{2,1,0:T(8,128)S(1)} %solve_first.1.fields_ref.before_ref), channel_id=1, source_target_pairs={{0,8},{8,0},{16,24},{24,16},{1,9},{9,1},{17,25},{25,17},{2,10},{10... | collective-permute-start | bytes 36872 | tf_op jit(solution)/shard_map/ppermute | solution.py:281
  31.6 1.4 %own_next.1 = (bf16[1024,256]{1,0:T(8,128)(2,1)S(1)}, f32[3,8,128]{2,1,0:T(8,128)S(1)}) custom-call(bf16[1024,256]{1,0:T(8,128)(2,1)S(1)} %bitcast.7, f32[3,8,128]{2,1,0:T(8,128)S(1)} %solve_first.1.fields_ref.before_ref), custom_call_target="tpu_custom_call" | custom-call | tf_op jit(solution)/shard_map/own_next/pallas_call | solution.py:328
  33.6 1.9 %pair_next.1.refs_0_ = f32[6,8,128]{2,1,0:T(8,128)S(1)} custom-call(s32[4,4]{1,0:T(4,128)S(1)} %slice_reduce_fusion.index_ref, s32[4,4]{1,0:T(4,128)S(1)} %bitcast.10, bf16[1024,256]{1,0:T(8,128)(2,1)S(1)} %get-tuple-element.12.own_ref, f32[3,8,128]{2,1,0:T(8,128)S(1)} %get-tuple-element.13.energy_ref, bf16[128,256]{1,0:T(8,128)(2,1)S(1)} %collective-permute-done.refs_0_, ...), custom_call_target="tpu_custom_call" | custom-call | tf_op jit(solution)/shard_map/pair_next/pallas_call | solution.py:336
  35.5 1.6 %collective-permute-start.18 = (f32[6,8,128]{2,1,0:T(8,128)S(1)}, f32[6,8,128]{2,1,0:T(8,128)S(1)}, u32[]{:S(2)}, u32[]{:S(2)}) collective-permute-start(f32[6,8,128]{2,1,0:T(8,128)S(1)} %pair_next.1.refs_0_), channel_id=1, source_target_pairs={{0,6},{1,7},{2,4},{3,5},{4,2},{5,3},{6,0},{7,1},{8,14},{9,15},{10,... | collective-permute-start | bytes 73736 | tf_op jit(solution)/shard_map/ppermute | solution.py:272
  37.6 1.5 %collective-permute-start.14 = (f32[6,8,128]{2,1,0:T(8,128)S(1)}, f32[6,8,128]{2,1,0:T(8,128)S(1)}, u32[]{:S(2)}, u32[]{:S(2)}) collective-permute-start(f32[6,8,128]{2,1,0:T(8,128)S(1)} %pair_next.1.refs_0_), channel_id=1, source_target_pairs={{0,2},{1,3},{2,0},{3,1},{4,6},{5,7},{6,4},{7,5},{8,10},{9,11},{10,... | collective-permute-start | bytes 73736 | tf_op jit(solution)/shard_map/ppermute | solution.py:272
  39.1 1.2 %collective-permute-done.18.refs_6_ = f32[6,8,128]{2,1,0:T(8,128)S(1)} collective-permute-done((f32[6,8,128]{2,1,0:T(8,128)S(1)}, f32[6,8,128]{2,1,0:T(8,128)S(1)}, u32[]{:S(2)}, u32[]{:S(2)}) %collective-permute-start.18) | collective-permute-done | bytes 24608 | tf_op jit(solution)/shard_map/ppermute | solution.py:272
  40.3 0.6 %collective-permute-done.16.refs_4_ = f32[6,8,128]{2,1,0:T(8,128)S(1)} collective-permute-done((f32[6,8,128]{2,1,0:T(8,128)S(1)}, f32[6,8,128]{2,1,0:T(8,128)S(1)}, u32[]{:S(2)}, u32[]{:S(2)}) %collective-permute-start.16) | collective-permute-done | bytes 24608 | tf_op jit(solution)/shard_map/ppermute | solution.py:272
  41.5 0.6 %collective-permute-done.17.refs_5_ = f32[6,8,128]{2,1,0:T(8,128)S(1)} collective-permute-done((f32[6,8,128]{2,1,0:T(8,128)S(1)}, f32[6,8,128]{2,1,0:T(8,128)S(1)}, u32[]{:S(2)}, u32[]{:S(2)}) %collective-permute-start.17) | collective-permute-done | bytes 24608 | tf_op jit(solution)/shard_map/ppermute | solution.py:275
  42.6 4.0 %solve_last.1 = (f32[3,8,128]{2,1,0:T(8,128)}, bf16[1024,256]{1,0:T(8,128)(2,1)}) custom-call(f32[3]{0:T(128)S(1)} %copy-done.3, f32[3,8,128]{2,1,0:T(8,128)S(1)} %solve_first.1.fields_ref.before_ref, bf16[1024,256]{1,0:T(8,128)(2,1)S(1)} %bitcast.8, f32[6,8,128]{2,1,0:T(8,128)S(1)} %pair_next.1.refs_0_, f32[6,8,128]{2,1,0:T(8,128)S(1)} %collective-permute-done.13.refs_1_, ...), custom_call_target="tpu_custom_call" | custom-call | tf_op jit(solution)/shard_map/solve_last/pallas_call | solution.py:345
  (32 shorter events, 4.2 us)
Async XLA Ops:
  1.5 1.1 %copy-start = (bf16[1,8,128,256]{3,2,1,0:T(8,128)(2,1)S(1)}, bf16[1,8,128,256]{3,2,1,0:T(8,128)(2,1)}, u32[]{:S(2)}) copy-start(bf16[1,8,128,256]{3,2,1,0:T(8,128)(2,1)} %param.4) | copy-start | bytes 1572868
  3.1 6.3 %collective-permute-start = (bf16[128,256]{1,0:T(8,128)(2,1)S(1)}, bf16[128,256]{1,0:T(8,128)(2,1)S(1)}, u32[]{:S(2)}, u32[]{:S(2)}) collective-permute-start(bf16[128,256]{1,0:T(8,128)(2,1)S(1)} %get-tuple-element.9), channel_id=1, source_target_pairs={{0,8},{8,0},{16,24},{24,16},{1,9},{9,1},{17,25},{25,17},{2,10},{10... | collective-permute-start | bytes 196616 | tf_op jit(solution)/shard_map/ppermute | solution.py:281
  6.3 7.3 %collective-permute-start.1 = (bf16[128,256]{1,0:T(8,128)(2,1)S(1)}, bf16[128,256]{1,0:T(8,128)(2,1)S(1)}, u32[]{:S(2)}, u32[]{:S(2)}) collective-permute-start(bf16[128,256]{1,0:T(8,128)(2,1)S(1)} %get-tuple-element.10), channel_id=1, source_target_pairs={{0,16},{8,24},{16,0},{24,8},{1,17},{9,25},{17,1},{25,9},{2,18},{10... | collective-permute-start | bytes 196616 | tf_op jit(solution)/shard_map/ppermute | solution.py:281
  8.8 6.1 %collective-permute-start.2 = (bf16[128,256]{1,0:T(8,128)(2,1)S(1)}, bf16[128,256]{1,0:T(8,128)(2,1)S(1)}, u32[]{:S(2)}, u32[]{:S(2)}) collective-permute-start(bf16[128,256]{1,0:T(8,128)(2,1)S(1)} %get-tuple-element.11), channel_id=1, source_target_pairs={{0,24},{8,16},{16,8},{24,0},{1,25},{9,17},{17,9},{25,1},{2,26},{10... | collective-permute-start | bytes 196616 | tf_op jit(solution)/shard_map/ppermute | solution.py:281
  8.9 6.1 %copy-start.2 = (s32[4,1,4]{2,1,0:T(1,128)S(1)}, s32[4,1,4]{2,1,0:T(1,128)}, u32[]{:S(2)}) copy-start(s32[4,1,4]{2,1,0:T(1,128)} %param.6) | copy-start | bytes 196
  9.4 22.2 %copy-start.1 = (bf16[1,8,128,256]{3,2,1,0:T(8,128)(2,1)S(1)}, bf16[1,8,128,256]{3,2,1,0:T(8,128)(2,1)}, u32[]{:S(2)}) copy-start(bf16[1,8,128,256]{3,2,1,0:T(8,128)(2,1)} %param.4) | copy-start | bytes 1572868
  14.9 9.4 %copy-start.3 = (f32[3]{0:T(128)S(1)}, f32[3]{0:T(128)}, u32[]{:S(2)}) copy-start(f32[3]{0:T(128)} %smoothing_ref.3) | copy-start | bytes 40
  16.2 4.8 %collective-permute-start.8 = (f32[6,8,128]{2,1,0:T(8,128)S(1)}, f32[6,8,128]{2,1,0:T(8,128)S(1)}, u32[]{:S(2)}, u32[]{:S(2)}) collective-permute-start(f32[6,8,128]{2,1,0:T(8,128)S(1)} %pair_first.1.refs_0_), channel_id=1, source_target_pairs={{0,6},{1,7},{2,4},{3,5},{4,2},{5,3},{6,0},{7,1},{8,14},{9,15},{10,... | collective-permute-start | bytes 73736 | tf_op jit(solution)/shard_map/ppermute | solution.py:272
  18.8 3.8 %collective-permute-start.6 = (f32[6,8,128]{2,1,0:T(8,128)S(1)}, f32[6,8,128]{2,1,0:T(8,128)S(1)}, u32[]{:S(2)}, u32[]{:S(2)}) collective-permute-start(f32[6,8,128]{2,1,0:T(8,128)S(1)} %pair_first.1.refs_0_), channel_id=1, source_target_pairs={{0,4},{1,5},{2,6},{3,7},{4,0},{5,1},{6,2},{7,3},{8,12},{9,13},{10,... | collective-permute-start | bytes 73736 | tf_op jit(solution)/shard_map/ppermute | solution.py:272
  19.3 3.8 %collective-permute-start.4 = (f32[6,8,128]{2,1,0:T(8,128)S(1)}, f32[6,8,128]{2,1,0:T(8,128)S(1)}, u32[]{:S(2)}, u32[]{:S(2)}) collective-permute-start(f32[6,8,128]{2,1,0:T(8,128)S(1)} %pair_first.1.refs_0_), channel_id=1, source_target_pairs={{0,2},{1,3},{2,0},{3,1},{4,6},{5,7},{6,4},{7,5},{8,10},{9,11},{10,... | collective-permute-start | bytes 73736 | tf_op jit(solution)/shard_map/ppermute | solution.py:272
  19.8 3.3 %collective-permute-start.3 = (f32[6,8,128]{2,1,0:T(8,128)S(1)}, f32[6,8,128]{2,1,0:T(8,128)S(1)}, u32[]{:S(2)}, u32[]{:S(2)}) collective-permute-start(f32[6,8,128]{2,1,0:T(8,128)S(1)} %pair_first.1.refs_0_), channel_id=1, source_target_pairs={{0,1},{1,0},{2,3},{3,2},{4,5},{5,4},{6,7},{7,6},{8,9},{9,8},{10,11... | collective-permute-start | bytes 73736 | tf_op jit(solution)/shard_map/ppermute | solution.py:275
  21.0 2.1 %collective-permute-start.9 = (f32[6,8,128]{2,1,0:T(8,128)S(1)}, f32[6,8,128]{2,1,0:T(8,128)S(1)}, u32[]{:S(2)}, u32[]{:S(2)}) collective-permute-start(f32[6,8,128]{2,1,0:T(8,128)S(1)} %collective-permute-done.8.refs_6_), channel_id=1, source_target_pairs={{0,1},{1,0},{2,3},{3,2},{4,5},{5,4},{6,7},{7,6},{8,9},{9,8},{10,11... | collective-permute-start | bytes 73736 | tf_op jit(solution)/shard_map/ppermute | solution.py:275
  22.6 1.2 %collective-permute-start.7 = (f32[6,8,128]{2,1,0:T(8,128)S(1)}, f32[6,8,128]{2,1,0:T(8,128)S(1)}, u32[]{:S(2)}, u32[]{:S(2)}) collective-permute-start(f32[6,8,128]{2,1,0:T(8,128)S(1)} %collective-permute-done.6.refs_4_), channel_id=1, source_target_pairs={{0,1},{1,0},{2,3},{3,2},{4,5},{5,4},{6,7},{7,6},{8,9},{9,8},{10,11... | collective-permute-start | bytes 73736 | tf_op jit(solution)/shard_map/ppermute | solution.py:275
  23.1 1.2 %collective-permute-start.5 = (f32[6,8,128]{2,1,0:T(8,128)S(1)}, f32[6,8,128]{2,1,0:T(8,128)S(1)}, u32[]{:S(2)}, u32[]{:S(2)}) collective-permute-start(f32[6,8,128]{2,1,0:T(8,128)S(1)} %collective-permute-done.4.refs_2_), channel_id=1, source_target_pairs={{0,1},{1,0},{2,3},{3,2},{4,5},{5,4},{6,7},{7,6},{8,9},{9,8},{10,11... | collective-permute-start | bytes 73736 | tf_op jit(solution)/shard_map/ppermute | solution.py:275
  27.1 5.9 %collective-permute-start.12 = (f32[3,8,128]{2,1,0:T(8,128)S(1)}, f32[3,8,128]{2,1,0:T(8,128)S(1)}, u32[]{:S(2)}, u32[]{:S(2)}) collective-permute-start(f32[3,8,128]{2,1,0:T(8,128)S(1)} %solve_first.1.fields_ref.before_ref), channel_id=1, source_target_pairs={{0,24},{8,16},{16,8},{24,0},{1,25},{9,17},{17,9},{25,1},{2,26},{10... | collective-permute-start | bytes 36872 | tf_op jit(solution)/shard_map/ppermute | solution.py:281
  29.0 4.6 %collective-permute-start.11 = (f32[3,8,128]{2,1,0:T(8,128)S(1)}, f32[3,8,128]{2,1,0:T(8,128)S(1)}, u32[]{:S(2)}, u32[]{:S(2)}) collective-permute-start(f32[3,8,128]{2,1,0:T(8,128)S(1)} %solve_first.1.fields_ref.before_ref), channel_id=1, source_target_pairs={{0,16},{8,24},{16,0},{24,8},{1,17},{9,25},{17,1},{25,9},{2,18},{10... | collective-permute-start | bytes 36872 | tf_op jit(solution)/shard_map/ppermute | solution.py:281
  29.0 4.6 %collective-permute-start.10 = (f32[3,8,128]{2,1,0:T(8,128)S(1)}, f32[3,8,128]{2,1,0:T(8,128)S(1)}, u32[]{:S(2)}, u32[]{:S(2)}) collective-permute-start(f32[3,8,128]{2,1,0:T(8,128)S(1)} %solve_first.1.fields_ref.before_ref), channel_id=1, source_target_pairs={{0,8},{8,0},{16,24},{24,16},{1,9},{9,1},{17,25},{25,17},{2,10},{10... | collective-permute-start | bytes 36872 | tf_op jit(solution)/shard_map/ppermute | solution.py:281
  35.5 4.8 %collective-permute-start.18 = (f32[6,8,128]{2,1,0:T(8,128)S(1)}, f32[6,8,128]{2,1,0:T(8,128)S(1)}, u32[]{:S(2)}, u32[]{:S(2)}) collective-permute-start(f32[6,8,128]{2,1,0:T(8,128)S(1)} %pair_next.1.refs_0_), channel_id=1, source_target_pairs={{0,6},{1,7},{2,4},{3,5},{4,2},{5,3},{6,0},{7,1},{8,14},{9,15},{10,... | collective-permute-start | bytes 73736 | tf_op jit(solution)/shard_map/ppermute | solution.py:272
  37.1 3.8 %collective-permute-start.16 = (f32[6,8,128]{2,1,0:T(8,128)S(1)}, f32[6,8,128]{2,1,0:T(8,128)S(1)}, u32[]{:S(2)}, u32[]{:S(2)}) collective-permute-start(f32[6,8,128]{2,1,0:T(8,128)S(1)} %pair_next.1.refs_0_), channel_id=1, source_target_pairs={{0,4},{1,5},{2,6},{3,7},{4,0},{5,1},{6,2},{7,3},{8,12},{9,13},{10,... | collective-permute-start | bytes 73736 | tf_op jit(solution)/shard_map/ppermute | solution.py:272
  37.6 3.8 %collective-permute-start.14 = (f32[6,8,128]{2,1,0:T(8,128)S(1)}, f32[6,8,128]{2,1,0:T(8,128)S(1)}, u32[]{:S(2)}, u32[]{:S(2)}) collective-permute-start(f32[6,8,128]{2,1,0:T(8,128)S(1)} %pair_next.1.refs_0_), channel_id=1, source_target_pairs={{0,2},{1,3},{2,0},{3,1},{4,6},{5,7},{6,4},{7,5},{8,10},{9,11},{10,... | collective-permute-start | bytes 73736 | tf_op jit(solution)/shard_map/ppermute | solution.py:272
  39.1 2.4 %collective-permute-start.13 = (f32[6,8,128]{2,1,0:T(8,128)S(1)}, f32[6,8,128]{2,1,0:T(8,128)S(1)}, u32[]{:S(2)}, u32[]{:S(2)}) collective-permute-start(f32[6,8,128]{2,1,0:T(8,128)S(1)} %pair_next.1.refs_0_), channel_id=1, source_target_pairs={{0,1},{1,0},{2,3},{3,2},{4,5},{5,4},{6,7},{7,6},{8,9},{9,8},{10,11... | collective-permute-start | bytes 73736 | tf_op jit(solution)/shard_map/ppermute | solution.py:275
  40.3 1.2 %collective-permute-start.19 = (f32[6,8,128]{2,1,0:T(8,128)S(1)}, f32[6,8,128]{2,1,0:T(8,128)S(1)}, u32[]{:S(2)}, u32[]{:S(2)}) collective-permute-start(f32[6,8,128]{2,1,0:T(8,128)S(1)} %collective-permute-done.18.refs_6_), channel_id=1, source_target_pairs={{0,1},{1,0},{2,3},{3,2},{4,5},{5,4},{6,7},{7,6},{8,9},{9,8},{10,11... | collective-permute-start | bytes 73736 | tf_op jit(solution)/shard_map/ppermute | solution.py:275
  40.9 1.2 %collective-permute-start.17 = (f32[6,8,128]{2,1,0:T(8,128)S(1)}, f32[6,8,128]{2,1,0:T(8,128)S(1)}, u32[]{:S(2)}, u32[]{:S(2)}) collective-permute-start(f32[6,8,128]{2,1,0:T(8,128)S(1)} %collective-permute-done.16.refs_4_), channel_id=1, source_target_pairs={{0,1},{1,0},{2,3},{3,2},{4,5},{5,4},{6,7},{7,6},{8,9},{9,8},{10,11... | collective-permute-start | bytes 73736 | tf_op jit(solution)/shard_map/ppermute | solution.py:275
  41.4 1.2 %collective-permute-start.15 = (f32[6,8,128]{2,1,0:T(8,128)S(1)}, f32[6,8,128]{2,1,0:T(8,128)S(1)}, u32[]{:S(2)}, u32[]{:S(2)}) collective-permute-start(f32[6,8,128]{2,1,0:T(8,128)S(1)} %collective-permute-done.14.refs_2_), channel_id=1, source_target_pairs={{0,1},{1,0},{2,3},{3,2},{4,5},{5,4},{6,7},{7,6},{8,9},{9,8},{10,11... | collective-permute-start | bytes 73736 | tf_op jit(solution)/shard_map/ppermute | solution.py:275

commit v2 on v0

v2 whole, which is shorter than its diff:
```python
import functools

import jax
import jax.numpy as jnp
from jax import lax
from jax.experimental import pallas as pl
from jax.experimental.pallas import tpu as pltpu
from jax.sharding import PartitionSpec as P

ROUNDS = 2
CG_ITERS = 3

damping = 0.05
sim_eps = 1e-05

f32 = jnp.float32
bf16 = jnp.bfloat16
VMEM = pl.BlockSpec(memory_space=pltpu.VMEM)
ANY = pl.BlockSpec(memory_space=pl.ANY)
PARAMS = pltpu.CompilerParams(vmem_limit_bytes=16 * 1024 * 1024)
NT = (((1,), (1,)), ((), ()))


def is_power(n):
    return n & (n - 1) == 0


def receiver(me, k, n):
    return me ^ k if is_power(n) else lax.rem(me + k, n)


def sender(me, k, n):
    return me ^ k if is_power(n) else lax.rem(me + n - k, n)


def survey_pairs(k, n):
    return [(i, i ^ k if is_power(n) else (i + k) % n) for i in range(n)]


def iota(shape, dim):
    return lax.broadcasted_iota(jnp.int32, shape, dim)


def time_of(sample, samples):
    return (sample.astype(f32) - (samples - 1) / 2.0) / (samples / 2.0)


def time_column(samples, lanes):
    return time_of(iota((samples, lanes), 0), samples)


def joined_blocks(data_ref, start, rows_x, rows_y):
    block = start // rows_y
    split = start - block * rows_y
    after = jnp.minimum(block + 1, rows_x - 1)
    here = data_ref[pl.ds(pl.multiple_of(block * rows_y, rows_y), rows_y), :].astype(f32)
    there = data_ref[pl.ds(pl.multiple_of(after * rows_y, rows_y), rows_y), :].astype(f32)
    return jnp.where(iota(here.shape, 0) >= split, here, there).astype(data_ref.dtype)


def pack_kernel(n, rows_x, index_ref, data_ref, *out_refs):
    me = lax.axis_index("survey")
    rows_y = data_ref.shape[0] // rows_x
    for k in range(1, n):
        start = jnp.min(index_ref[me, pl.ds(receiver(me, k, n), 1), :])
        out_refs[k - 1][...] = joined_blocks(data_ref, start, rows_x, rows_y)


def put_rows(ref, k, rows):
    for i, row in enumerate(rows):
        ref[k, i : i + 1, :] = row


def mean_over(values):
    return jnp.sum(values, axis=0, keepdims=True) * (1.0 / values.shape[0])


def energy_rows(vals, moved, time_pos):
    tilted = time_pos * vals
    return [mean_over(moved * moved), mean_over(vals * vals), mean_over(tilted * tilted)]


def prepare_kernel(n, index_ref, count_ref, data_ref, basis_ref, own_ref, moved_ref, mask_ref, energy_ref):
    me = lax.axis_index("survey")
    samples, rows_y = own_ref.shape[1:]
    rows_x = data_ref.shape[0] // rows_y
    row, col = iota((samples, samples), 0), iota((samples, samples), 1)
    basis_ref[:samples, :] = jnp.where(row == col, 1.0, 0.0).astype(bf16)
    basis_ref[samples:, :] = (jnp.where(col == row + 1, 0.5, 0.0) - jnp.where(col == row - 1, 0.5, 0.0)).astype(bf16)
    time_pos = time_column(samples, rows_y)
    position = iota((rows_x, rows_y), 0) * rows_y + iota((rows_x, rows_y), 1)
    for k in range(1, n):
        source = sender(me, k, n)
        start = jnp.min(index_ref[source, pl.ds(me, 1), :])
        counts = count_ref[source]
        count = jnp.sum(jnp.where(iota(counts.shape, 1) == me, counts, 0))
        mask_ref[k - 1] = jnp.where((position >= start) & (position < start + count), 1.0, 0.0)
        rows = joined_blocks(data_ref, start, rows_x, rows_y)
        both = lax.dot_general(basis_ref[...], rows, NT, preferred_element_type=f32)
        own_ref[k - 1] = both[:samples]
        moved_ref[k - 1] = both[samples:]
        put_rows(energy_ref, k - 1, energy_rows(both[:samples], both[samples:], time_pos))


def corrected_lanes(values, moved, fields_ref, mask, time_pos):
    shift, gain, trend = [jnp.sum(fields_ref[c] * mask, axis=0, keepdims=True) for c in range(3)]
    amplitude = jnp.exp(gain + trend * time_pos)
    return (amplitude * (values + shift * moved)).astype(bf16)


def refresh_kernel(n, fields_ref, basis_ref, own_ref, moved_ref, mask_ref, *refs):
    arrived = refs[: n - 1]
    new_own_ref, new_moved_ref, energy_ref, partner_ref, partner_moved_ref = refs[n - 1 :]
    samples, rows_y = own_ref.shape[1:]
    time_pos = time_column(samples, rows_y)
    for k in range(n - 1):
        rounded = corrected_lanes(own_ref[k], moved_ref[k], fields_ref, mask_ref[k], time_pos)
        vals = rounded.astype(f32)
        moved = jnp.dot(basis_ref[samples:, :], rounded, preferred_element_type=f32)
        new_own_ref[k] = vals
        new_moved_ref[k] = moved
        put_rows(energy_ref, k, energy_rows(vals, moved, time_pos))
        both = lax.dot_general(basis_ref[...], arrived[k][...], NT, preferred_element_type=f32)
        partner_ref[k] = both[:samples]
        partner_moved_ref[k] = both[samples:]


def add_pair(sums, own, moved, partner, mask, energy_ref, k, time_pos):
    residual = partner - own
    along = residual * own
    slope_sum = mean_over(residual * moved)
    gain_sum = mean_over(along)
    trend_sum = mean_over(time_pos * along)
    cross_term = mean_over(own * partner)
    other_energy = mean_over(partner * partner)
    energy = [energy_ref[k, i : i + 1, :] for i in range(3)]
    weight = cross_term * cross_term / ((energy[1] + sim_eps) * (other_energy + sim_eps))
    for c, row in enumerate([slope_sum, gain_sum, trend_sum] + energy):
        term = mask * (weight * row)
        sums[c] = term if sums[c] is None else sums[c] + term


def pair_first_kernel(n, basis_ref, own_ref, moved_ref, mask_ref, energy_ref, *refs):
    arrived, out_ref = refs[: n - 1], refs[-1]
    samples, rows_y = own_ref.shape[1:]
    time_pos = time_column(samples, rows_y)
    sums = [None] * 6
    for k in range(n - 1):
        partner = lax.dot_general(basis_ref[:samples, :], arrived[k][...], NT, preferred_element_type=f32)
        add_pair(sums, own_ref[k], moved_ref[k], partner, mask_ref[k], energy_ref, k, time_pos)
    for c in range(6):
        out_ref[c] = sums[c]


def pair_next_kernel(n, own_ref, moved_ref, mask_ref, energy_ref, partner_ref, partner_moved_ref, *refs):
    field_refs, out_ref = refs[: n - 1], refs[-1]
    samples, rows_y = own_ref.shape[1:]
    time_pos = time_column(samples, rows_y)
    sums = [None] * 6
    for k in range(n - 1):
        partner = corrected_lanes(partner_ref[k], partner_moved_ref[k], field_refs[k], mask_ref[k], time_pos)
        add_pair(sums, own_ref[k], moved_ref[k], partner.astype(f32), mask_ref[k], energy_ref, k, time_pos)
    for c in range(6):
        out_ref[c] = sums[c]


def grid_solve(masks, smoothing_ref, piece_refs, grid_ref, tile):
    rows_x = piece_refs[0].shape[1]
    for piece, mask in zip(piece_refs, masks):
        spot = pl.multiple_of((tile ^ mask) * rows_x, rows_x)
        for c in range(6):
            grid_ref[c, pl.ds(spot, rows_x), :] = piece[c]
    size_x, size_y = grid_ref.shape[1:]
    grid_x = iota((size_x, size_y), 0)
    grid_y = iota((size_x, size_y), 1)
    each = range(3)

    def total(q):
        return jnp.sum(jnp.sum(q, axis=0, keepdims=True), axis=1, keepdims=True)

    def beside(v):
        return (
            jnp.where(grid_x > 0, pltpu.roll(v, 1, 0), 0.0)
            + jnp.where(grid_x < size_x - 1, pltpu.roll(v, size_x - 1, 0), 0.0)
            + jnp.where(grid_y > 0, pltpu.roll(v, 1, 1), 0.0)
            + jnp.where(grid_y < size_y - 1, pltpu.roll(v, size_y - 1, 1), 0.0)
        )

    strength = [smoothing_ref[0:1, c : c + 1] for c in each]
    diagonal = [grid_ref[3 + c] + (damping + 4.0 * strength[c]) for c in each]

    def apply(v):
        near = [beside(v[c]) for c in each]
        return [diagonal[c] * v[c] - strength[c] * near[c] for c in each]

    residual = [grid_ref[c] for c in each]
    image = apply(residual)
    norm_now = [total(residual[c] * residual[c]) for c in each]
    product = [total(residual[c] * image[c]) for c in each]
    alpha = [norm_now[c] / product[c] for c in each]
    direction, along = residual, image
    update = [alpha[c] * direction[c] for c in each]
    for iteration in range(1, CG_ITERS):
        residual = [residual[c] - alpha[c] * along[c] for c in each]
        image = apply(residual)
        norm_next = [total(residual[c] * residual[c]) for c in each]
        product = [total(residual[c] * image[c]) for c in each]
        ratio = [norm_next[c] / norm_now[c] for c in each]
        alpha = [norm_next[c] / (product[c] - ratio[c] * norm_next[c] / alpha[c]) for c in each]
        direction = [residual[c] + ratio[c] * direction[c] for c in each]
        if iteration + 1 < CG_ITERS:
            along = [image[c] + ratio[c] * along[c] for c in each]
        update = [update[c] + alpha[c] * direction[c] for c in each]
        norm_now = norm_next
    return update


def own_part(updates, grid_ref, tile, rows_x):
    for c in range(3):
        grid_ref[c] = updates[c]
    spot = pl.ds(pl.multiple_of(tile * rows_x, rows_x), rows_x)
    return [grid_ref[c, spot, :] for c in range(3)]


def solve_first_kernel(masks, smoothing_ref, *refs):
    pieces, fields_ref, grid_ref = refs[: len(masks)], refs[-2], refs[-1]
    tile = lax.axis_index("tile")
    updates = grid_solve(masks, smoothing_ref, pieces, grid_ref, tile)
    for c, mine in enumerate(own_part(updates, grid_ref, tile, fields_ref.shape[1])):
        fields_ref[c] = mine


def three_parts(values):
    parts = []
    for _ in range(3):
        part = values.astype(bf16).astype(f32)
        parts.append(part)
        values = values - part
    return parts


def solve_last_kernel(masks, smoothing_ref, before_ref, data_ref, basis_ref, *refs):
    pieces = refs[: len(masks)]
    fields_ref, volume_ref, grid_ref, block_ref, sems = refs[len(masks) :]
    tile = lax.axis_index("tile")
    updates = grid_solve(masks, smoothing_ref, pieces, grid_ref, tile)
    rows_x, rows_y = fields_ref.shape[1:]
    samples = data_ref.shape[1]
    parts = []
    for c, mine in enumerate(own_part(updates, grid_ref, tile, rows_x)):
        mine = before_ref[c] + mine
        fields_ref[c] = mine
        parts += three_parts(mine)
    lanes = 16 * rows_x
    parts.append(jnp.zeros((lanes - 9 * rows_x, rows_y), f32))
    columns = jnp.transpose(jnp.concatenate(parts, axis=0))
    kind = iota((lanes, samples), 0) // rows_x
    spread_shift = jnp.where(kind < 3, 1.0, 0.0).astype(bf16)
    time_pos = time_of(iota((lanes, samples), 1), samples)
    spread_power = jnp.where((kind >= 3) & (kind < 6), 1.0, jnp.where((kind >= 6) & (kind < 9), time_pos, 0.0)).astype(bf16)
    which = lax.rem(iota((rows_y, lanes), 1), rows_x)
    copies = []
    for x in range(rows_x):
        rows = slice(x * rows_y, (x + 1) * rows_y)
        mine = jnp.where(which == x, columns, 0.0).astype(bf16)
        shift = jnp.dot(mine, spread_shift, preferred_element_type=f32)
        power = jnp.dot(mine, spread_power, preferred_element_type=f32)
        raw = data_ref[rows, :]
        slope = lax.dot_general(raw, basis_ref[samples:, :], NT, preferred_element_type=f32)
        block_ref[rows, :] = (jnp.exp(power) * (raw.astype(f32) + shift * slope)).astype(volume_ref.dtype)
        copy = pltpu.make_async_copy(block_ref.at[rows, :], volume_ref.at[rows, :], sems.at[x])
        copy.start()
        copies.append(copy)
    for copy in copies:
        copy.wait()


def gather_tiles(piece, n):
    if not is_power(n):
        every = lax.all_gather(piece, "tile")
        me = lax.axis_index("tile")
        return list(range(n)), [lax.dynamic_index_in_dim(every, me ^ m, keepdims=False) for m in range(n)]
    pieces = {0: piece}
    for mask in range(2, n, 2):
        pieces[mask] = lax.ppermute(piece, "tile", [(i, i ^ mask) for i in range(n)])
    if n > 1:
        for mask in list(pieces):
            pieces[mask + 1] = lax.ppermute(pieces[mask], "tile", [(i, i ^ 1) for i in range(n)])
    masks = sorted(pieces)
    return masks, [pieces[m] for m in masks]


def exchange(arrays, n):
    return [lax.ppermute(a, "survey", survey_pairs(k, n)) for k, a in zip(range(1, n), arrays)]


def call(kernel, name, out_shape, n_in, **options):
    single = not isinstance(out_shape, list)
    options = {"out_specs": VMEM if single else [VMEM] * len(out_shape), **options}
    return pl.pallas_call(
        kernel,
        out_shape=out_shape,
        in_specs=[VMEM] * n_in,
        compiler_params=PARAMS,
        name=name,
        **options,
    )


def local(n_survey, n_tile, data, correlation_index, correlation_count, smoothing):
    rows_x, rows_y, samples = data.shape[1:]
    total, cap = rows_x * rows_y, correlation_index.shape[-1]
    assert cap <= rows_y and is_power(n_tile)
    others = n_survey - 1
    raw = data.reshape(total, samples)
    index = correlation_index[:, 0]
    smoothing = smoothing.reshape(1, 3)
    packed = jax.ShapeDtypeStruct((rows_y, samples), data.dtype)
    field_shape = jax.ShapeDtypeStruct((3, rows_x, rows_y), f32)
    term_shape = jax.ShapeDtypeStruct((6, rows_x, rows_y), f32)
    lane_shape = jax.ShapeDtypeStruct((others, samples, rows_y), f32)
    mask_shape = jax.ShapeDtypeStruct((others, rows_x, rows_y), f32)
    energy_shape = jax.ShapeDtypeStruct((others, 8, rows_y), f32)
    basis_shape = jax.ShapeDtypeStruct((2 * samples, samples), bf16)
    volume_shape = jax.ShapeDtypeStruct((total, samples), data.dtype)
    grid = pltpu.VMEM((6, rows_x * n_tile, rows_y), f32)

    outgoing = call(functools.partial(pack_kernel, n_survey, rows_x), "pack", [packed] * others, 2)(index, raw)
    arrived = exchange(outgoing, n_survey)
    basis, own, moved, mask, energy = call(
        functools.partial(prepare_kernel, n_survey),
        "prepare",
        [basis_shape, lane_shape, lane_shape, mask_shape, energy_shape],
        3,
    )(index, correlation_count, raw)
    terms = call(functools.partial(pair_first_kernel, n_survey), "pair_first", term_shape, 5 + others)(
        basis, own, moved, mask, energy, *arrived
    )
    masks, pieces = gather_tiles(terms, n_tile)
    fields = call(
        functools.partial(solve_first_kernel, masks), "solve_first", field_shape, 1 + n_tile, scratch_shapes=[grid]
    )(smoothing, *pieces)

    partner_fields = exchange([fields] * others, n_survey)
    own, moved, energy, partner, partner_moved = call(
        functools.partial(refresh_kernel, n_survey),
        "refresh",
        [lane_shape, lane_shape, energy_shape, lane_shape, lane_shape],
        5 + others,
    )(fields, basis, own, moved, mask, *arrived)
    terms = call(functools.partial(pair_next_kernel, n_survey), "pair_next", term_shape, 6 + others)(
        own, moved, mask, energy, partner, partner_moved, *partner_fields
    )
    masks, pieces = gather_tiles(terms, n_tile)
    fields, volume = call(
        functools.partial(solve_last_kernel, masks),
        "solve_last",
        [field_shape, volume_shape],
        4 + n_tile,
        out_specs=[VMEM, ANY],
        scratch_shapes=[grid, pltpu.VMEM((total, samples), data.dtype), pltpu.SemaphoreType.DMA((rows_x,))],
    )(smoothing, fields, raw, basis, *pieces)
    return fields.reshape(1, 3, rows_x, rows_y), volume.reshape(1, rows_x, rows_y, samples)


def solution(mesh):
    placed = (
        P("survey", "tile", None, None),
        P(None, "tile", None, None),
        P(None, "tile", None),
        P(),
    )
    return jax.shard_map(
        functools.partial(local, mesh.shape["survey"], mesh.shape["tile"]),
        mesh=mesh,
        in_specs=placed,
        out_specs=(P("survey", None, "tile", None), P("survey", "tile", None, None)),
        check_vma=False,
    )
```

time: 181 us -> 42.8 us (0.24); the launches traced: 179 us -> 42.6 us
  blocking collectives: 92.5 us -> 0 us
  other arithmetic: 23 us -> 0 us
  waiting for transfers between devices: 26.3 us -> 16.9 us
  local copies, waits for them, and re-layouts: 10.1 us -> 1.75 us
  starting transfers between devices: 25.6 us -> 17.6 us
  Pallas kernels: 0 us -> 5.62 us
    psum x6 -> x0, blocking collectives: 92.5 us -> none  [paired(): lax.psum((jnp.sum(residual * residual, axis=(1, 2)), jnp.sum(residual * i...]
    all_to_all x2 -> x0, waiting for transfers between devices: 12.3 us -> none  [send_traces(): lax.all_to_all(outgoing, 'survey', split_axis=0, concat_axis=0, tiled=True)]
    all_to_all x2 -> x0, starting transfers between devices: 9.93 us -> none  [send_traces(): lax.all_to_all(outgoing, 'survey', split_axis=0, concat_axis=0, tiled=True)]
    scatter-add x4 -> x0, other arithmetic: 9.52 us -> none  [the longest x2 4.76 us: solve_round(): empty_sum.at[:, recv_index].add(numerator).reshape(3, rows_x, rows_y)]
    gather x4 -> x0, local copies, waits for them, and re-layouts: 7.81 us -> none  [the longest x2 3.91 us: send_traces(): outgoing = jnp.take(current, send_index, axis=0)]
    pallas_call x0 -> x7, Pallas kernels: none -> 5.62 us  [the longest x1 2.81 us: local(): call(functools.partial(solve_last_kernel, masks), 'solve_last', [field_sh...]
    convert_element_type x6 -> x0, other arithmetic: 4.99 us -> none  [the longest x3 3.59 us: corrected(): (amplitude * (values + time_shift[..., None] * time_slope(values))).astyp...]
    reduce_sum x10 -> x0, other arithmetic: 3.98 us -> none  [the longest x2 2.61 us: pair_terms(): cross_term = jnp.mean(own_vals * partner_vals, axis=-1)]
  transfers between devices with their start and end apart: 14 -> 20, of which waited for: 8 -> 11; matrix products, arithmetic and copies ran while one was open for 6% -> 0% of each run, Pallas kernels for 0% -> 3%
where the time goes in v2:
time: 42.8 us; the launch traced here: 42.6 us
  starting transfers between devices  17.6 us (41%)
  waiting for transfers between devices  16.9 us (39%)
  Pallas kernels  5.62 us (13%)
  local copies, waits for them, and re-layouts  1.75 us (4%)
  between operations  0.76 us (2%)
    ppermute x6, starting transfers between devices, exchange(): lax.ppermute(a, 'survey', survey_pairs(k, n))  10.2 us
    ppermute x6, waiting for transfers between devices, exchange(): lax.ppermute(a, 'survey', survey_pairs(k, n))  8.34 us
    ppermute x6, starting transfers between devices, gather_tiles(): lax.ppermute(piece, 'tile', [(i, i ^ mask) for i in range(n)])  7.1 us
    ppermute x6, waiting for transfers between devices, gather_tiles(): lax.ppermute(piece, 'tile', [(i, i ^ mask) for i in range(n)])  6.17 us
    pallas_call x1, Pallas kernels, local(): call(functools.partial(solve_last_kernel, masks), 'solve_last', [field_sh...  2.81 us
    ppermute x8, waiting for transfers between devices, gather_tiles(): lax.ppermute(pieces[mask], 'tile', [(i, i ^ 1) for i in range(n)])  2.36 us
    unnamed x10, local copies, waits for them, and re-layouts  1.75 us
  transfers between devices with their start and end apart: 20, of which 11 were waited for; matrix products, arithmetic and copies ran while one was open for 0% of the time, Pallas kernels for 3%

profile of v2, /device:TPU:0, one launch (start us, length us, event | category | flops | bytes accessed | tf_op | source)
XLA Modules:
  0.0 42.6 jit_solution(17981724661381746731)
XLA Ops:
  0.6 1.0 %copy-done = bf16[1,8,128,256]{3,2,1,0:T(8,128)(2,1)S(1)} copy-done((bf16[1,8,128,256]{3,2,1,0:T(8,128)(2,1)S(1)}, bf16[1,8,128,256]{3,2,1,0:T(8,128)(2,1)}, u32[]{:S(2)}) %copy-start) | copy-done | bytes 524312
  1.7 0.7 %copy-done.2 = s32[4,1,4,128]{3,2,1,0:T(4,128)S(1)} copy-done((s32[4,1,4,128]{3,2,1,0:T(4,128)S(1)}, s32[4,1,4,128]{3,2,1,0:T(4,128)}, u32[]{:S(2)}) %copy-start.2) | copy-done | bytes 8216
  2.7 3.1 %collective-permute-start = (bf16[128,256]{1,0:T(8,128)(2,1)S(1)}, bf16[128,256]{1,0:T(8,128)(2,1)S(1)}, u32[]{:S(2)}, u32[]{:S(2)}) collective-permute-start(bf16[128,256]{1,0:T(8,128)(2,1)S(1)} %get-tuple-element.22), channel_id=1, source_target_pairs={{0,8},{8,0},{16,24},{24,16},{1,9},{9,1},{17,25},{25,17},{2,10},{10... | collective-permute-start | bytes 196616 | tf_op jit(solution)/shard_map/ppermute | solution.py:294
  5.8 2.6 %collective-permute-start.1 = (bf16[128,256]{1,0:T(8,128)(2,1)S(1)}, bf16[128,256]{1,0:T(8,128)(2,1)S(1)}, u32[]{:S(2)}, u32[]{:S(2)}) collective-permute-start(bf16[128,256]{1,0:T(8,128)(2,1)S(1)} %get-tuple-element.23), channel_id=1, source_target_pairs={{0,16},{8,24},{16,0},{24,8},{1,17},{9,25},{17,1},{25,9},{2,18},{10... | collective-permute-start | bytes 196616 | tf_op jit(solution)/shard_map/ppermute | solution.py:294
  8.4 0.6 %prepare.1 = (bf16[512,256]{1,0:T(8,128)(2,1)S(1)}, f32[3,256,128]{2,1,0:T(8,128)S(1)}, f32[3,256,128]{2,1,0:T(8,128)S(1)}, f32[3,8,128]{2,1,0:T(8,128)S(1)}, f32[3,8,128]{2,1,0:T(8,128)S(1)}) custom-call(s32[4,4,128]{2,1,0:T(4,128)S(1)} %bitcast.9, s32[4,1,4]{2,1,0:T(1,128)S(1)} %copy-done.4, bf16[1024,256]{1,0:T(8,128)(2,1)S(1)} %bitcast.6), custom_call_target="tpu_custom_call" | custom-call | tf_op jit(solution)/shard_map/prepare/pallas_call | solution.py:330
  9.0 4.0 %collective-permute-done.1.refs_1_ = bf16[128,256]{1,0:T(8,128)(2,1)S(1)} collective-permute-done((bf16[128,256]{1,0:T(8,128)(2,1)S(1)}, bf16[128,256]{1,0:T(8,128)(2,1)S(1)}, u32[]{:S(2)}, u32[]{:S(2)}) %collective-permute-start.1) | collective-permute-done | bytes 65568 | tf_op jit(solution)/shard_map/ppermute | solution.py:294
  13.0 1.4 %collective-permute-done.2.refs_2_ = bf16[128,256]{1,0:T(8,128)(2,1)S(1)} collective-permute-done((bf16[128,256]{1,0:T(8,128)(2,1)S(1)}, bf16[128,256]{1,0:T(8,128)(2,1)S(1)}, u32[]{:S(2)}, u32[]{:S(2)}) %collective-permute-start.2) | collective-permute-done | bytes 65568 | tf_op jit(solution)/shard_map/ppermute | solution.py:294
  14.8 1.6 %collective-permute-start.4 = (f32[6,8,128]{2,1,0:T(8,128)S(1)}, f32[6,8,128]{2,1,0:T(8,128)S(1)}, u32[]{:S(2)}, u32[]{:S(2)}) collective-permute-start(f32[6,8,128]{2,1,0:T(8,128)S(1)} %pair_first.1.refs_0_), channel_id=1, source_target_pairs={{0,2},{1,3},{2,0},{3,1},{4,6},{5,7},{6,4},{7,5},{8,10},{9,11},{10,... | collective-permute-start | bytes 73736 | tf_op jit(solution)/shard_map/ppermute | solution.py:285
  16.4 1.5 %collective-permute-start.6 = (f32[6,8,128]{2,1,0:T(8,128)S(1)}, f32[6,8,128]{2,1,0:T(8,128)S(1)}, u32[]{:S(2)}, u32[]{:S(2)}) collective-permute-start(f32[6,8,128]{2,1,0:T(8,128)S(1)} %pair_first.1.refs_0_), channel_id=1, source_target_pairs={{0,4},{1,5},{2,6},{3,7},{4,0},{5,1},{6,2},{7,3},{8,12},{9,13},{10,... | collective-permute-start | bytes 73736 | tf_op jit(solution)/shard_map/ppermute | solution.py:285
  17.9 0.5 %collective-permute-start.8 = (f32[6,8,128]{2,1,0:T(8,128)S(1)}, f32[6,8,128]{2,1,0:T(8,128)S(1)}, u32[]{:S(2)}, u32[]{:S(2)}) collective-permute-start(f32[6,8,128]{2,1,0:T(8,128)S(1)} %pair_first.1.refs_0_), channel_id=1, source_target_pairs={{0,6},{1,7},{2,4},{3,5},{4,2},{5,3},{6,0},{7,1},{8,14},{9,15},{10,... | collective-permute-start | bytes 73736 | tf_op jit(solution)/shard_map/ppermute | solution.py:285
  18.9 1.3 %collective-permute-done.6.refs_4_ = f32[6,8,128]{2,1,0:T(8,128)S(1)} collective-permute-done((f32[6,8,128]{2,1,0:T(8,128)S(1)}, f32[6,8,128]{2,1,0:T(8,128)S(1)}, u32[]{:S(2)}, u32[]{:S(2)}) %collective-permute-start.6) | collective-permute-done | bytes 24608 | tf_op jit(solution)/shard_map/ppermute | solution.py:285
  20.2 2.4 %collective-permute-done.8.refs_6_ = f32[6,8,128]{2,1,0:T(8,128)S(1)} collective-permute-done((f32[6,8,128]{2,1,0:T(8,128)S(1)}, f32[6,8,128]{2,1,0:T(8,128)S(1)}, u32[]{:S(2)}, u32[]{:S(2)}) %collective-permute-start.8) | collective-permute-done | bytes 24608 | tf_op jit(solution)/shard_map/ppermute | solution.py:285
  22.6 1.2 %collective-permute-done.9.refs_7_ = f32[6,8,128]{2,1,0:T(8,128)S(1)} collective-permute-done((f32[6,8,128]{2,1,0:T(8,128)S(1)}, f32[6,8,128]{2,1,0:T(8,128)S(1)}, u32[]{:S(2)}, u32[]{:S(2)}) %collective-permute-start.9) | collective-permute-done | bytes 24608 | tf_op jit(solution)/shard_map/ppermute | solution.py:288
  23.8 0.7 %solve_first.1.fields_ref.before_ref = f32[3,8,128]{2,1,0:T(8,128)S(1)} custom-call(f32[1,3]{1,0:T(1,128)S(1)} %bitcast.10, f32[6,8,128]{2,1,0:T(8,128)S(1)} %pair_first.1.refs_0_, f32[6,8,128]{2,1,0:T(8,128)S(1)} %collective-permute-done.3.refs_1_, f32[6,8,128]{2,1,0:T(8,128)S(1)} %collective-permute-done.4.refs_2_, ...), custom_call_target="tpu_custom_call" | custom-call | tf_op jit(solution)/shard_map/solve_first/pallas_call | solution.py:340
  24.6 2.3 %collective-permute-start.11 = (f32[3,8,128]{2,1,0:T(8,128)S(1)}, f32[3,8,128]{2,1,0:T(8,128)S(1)}, u32[]{:S(2)}, u32[]{:S(2)}) collective-permute-start(f32[3,8,128]{2,1,0:T(8,128)S(1)} %solve_first.1.fields_ref.before_ref), channel_id=1, source_target_pairs={{0,16},{8,24},{16,0},{24,8},{1,17},{9,25},{17,1},{25,9},{2,18},{10... | collective-permute-start | bytes 36872 | tf_op jit(solution)/shard_map/ppermute | solution.py:294
  26.9 2.0 %collective-permute-start.12 = (f32[3,8,128]{2,1,0:T(8,128)S(1)}, f32[3,8,128]{2,1,0:T(8,128)S(1)}, u32[]{:S(2)}, u32[]{:S(2)}) collective-permute-start(f32[3,8,128]{2,1,0:T(8,128)S(1)} %solve_first.1.fields_ref.before_ref), channel_id=1, source_target_pairs={{0,24},{8,16},{16,8},{24,0},{1,25},{9,17},{17,9},{25,1},{2,26},{10... | collective-permute-start | bytes 36872 | tf_op jit(solution)/shard_map/ppermute | solution.py:294
  28.9 0.5 %refresh.1 = (f32[3,256,128]{2,1,0:T(8,128)S(1)}, f32[3,256,128]{2,1,0:T(8,128)S(1)}, f32[3,8,128]{2,1,0:T(8,128)S(1)}, f32[3,256,128]{2,1,0:T(8,128)S(1)}, f32[3,256,128]{2,1,0:T(8,128)S(1)}) custom-call(f32[3,8,128]{2,1,0:T(8,128)S(1)} %solve_first.1.fields_ref.before_ref, bf16[512,256]{1,0:T(8,128)(2,1)S(1)} %get-tuple-element.17.basis_ref, ...), custom_call_target="tpu_custom_call" | custom-call | tf_op jit(solution)/shard_map/refresh/pallas_call | solution.py:345
  29.5 2.9 %collective-permute-done.12.refs_2_ = f32[3,8,128]{2,1,0:T(8,128)S(1)} collective-permute-done((f32[3,8,128]{2,1,0:T(8,128)S(1)}, f32[3,8,128]{2,1,0:T(8,128)S(1)}, u32[]{:S(2)}, u32[]{:S(2)}) %collective-permute-start.12) | collective-permute-done | bytes 12320 | tf_op jit(solution)/shard_map/ppermute | solution.py:294
  32.8 0.6 %collective-permute-start.14 = (f32[6,8,128]{2,1,0:T(8,128)S(1)}, f32[6,8,128]{2,1,0:T(8,128)S(1)}, u32[]{:S(2)}, u32[]{:S(2)}) collective-permute-start(f32[6,8,128]{2,1,0:T(8,128)S(1)} %pair_next.1.refs_0_), channel_id=1, source_target_pairs={{0,2},{1,3},{2,0},{3,1},{4,6},{5,7},{6,4},{7,5},{8,10},{9,11},{10,... | collective-permute-start | bytes 73736 | tf_op jit(solution)/shard_map/ppermute | solution.py:285
  33.4 0.5 %collective-permute-start.16 = (f32[6,8,128]{2,1,0:T(8,128)S(1)}, f32[6,8,128]{2,1,0:T(8,128)S(1)}, u32[]{:S(2)}, u32[]{:S(2)}) collective-permute-start(f32[6,8,128]{2,1,0:T(8,128)S(1)} %pair_next.1.refs_0_), channel_id=1, source_target_pairs={{0,4},{1,5},{2,6},{3,7},{4,0},{5,1},{6,2},{7,3},{8,12},{9,13},{10,... | collective-permute-start | bytes 73736 | tf_op jit(solution)/shard_map/ppermute | solution.py:285
  33.9 2.4 %collective-permute-start.18 = (f32[6,8,128]{2,1,0:T(8,128)S(1)}, f32[6,8,128]{2,1,0:T(8,128)S(1)}, u32[]{:S(2)}, u32[]{:S(2)}) collective-permute-start(f32[6,8,128]{2,1,0:T(8,128)S(1)} %pair_next.1.refs_0_), channel_id=1, source_target_pairs={{0,6},{1,7},{2,4},{3,5},{4,2},{5,3},{6,0},{7,1},{8,14},{9,15},{10,... | collective-permute-start | bytes 73736 | tf_op jit(solution)/shard_map/ppermute | solution.py:285
  37.2 1.4 %collective-permute-done.18.refs_6_ = f32[6,8,128]{2,1,0:T(8,128)S(1)} collective-permute-done((f32[6,8,128]{2,1,0:T(8,128)S(1)}, f32[6,8,128]{2,1,0:T(8,128)S(1)}, u32[]{:S(2)}, u32[]{:S(2)}) %collective-permute-start.18) | collective-permute-done | bytes 24608 | tf_op jit(solution)/shard_map/ppermute | solution.py:285
  38.6 1.2 %collective-permute-done.19.refs_7_ = f32[6,8,128]{2,1,0:T(8,128)S(1)} collective-permute-done((f32[6,8,128]{2,1,0:T(8,128)S(1)}, f32[6,8,128]{2,1,0:T(8,128)S(1)}, u32[]{:S(2)}, u32[]{:S(2)}) %collective-permute-start.19) | collective-permute-done | bytes 24608 | tf_op jit(solution)/shard_map/ppermute | solution.py:288
  39.8 2.8 %solve_last.1 = (f32[3,8,128]{2,1,0:T(8,128)}, bf16[1024,256]{1,0:T(8,128)(2,1)}) custom-call(f32[1,3]{1,0:T(1,128)S(1)} %bitcast.11, f32[3,8,128]{2,1,0:T(8,128)S(1)} %solve_first.1.fields_ref.before_ref, bf16[1024,256]{1,0:T(8,128)(2,1)S(1)} %bitcast.7, bf16[512,256]{1,0:T(8,128)(2,1)S(1)} %get-tuple-element.17.basis_ref, ...), custom_call_target="tpu_custom_call" | custom-call | tf_op jit(solution)/shard_map/solve_last/pallas_call | solution.py:355
  (33 shorter events, 2.5 us)
Async XLA Ops:
  0.6 1.0 %copy-start = (bf16[1,8,128,256]{3,2,1,0:T(8,128)(2,1)S(1)}, bf16[1,8,128,256]{3,2,1,0:T(8,128)(2,1)}, u32[]{:S(2)}) copy-start(bf16[1,8,128,256]{3,2,1,0:T(8,128)(2,1)} %param.4) | copy-start | bytes 1572868
  2.4 6.0 %copy-start.1 = (bf16[1,8,128,256]{3,2,1,0:T(8,128)(2,1)S(1)}, bf16[1,8,128,256]{3,2,1,0:T(8,128)(2,1)}, u32[]{:S(2)}) copy-start(bf16[1,8,128,256]{3,2,1,0:T(8,128)(2,1)} %param.4) | copy-start | bytes 1572868
  2.6 5.7 %copy-start.4 = (s32[4,1,4]{2,1,0:T(1,128)S(1)}, s32[4,1,4]{2,1,0:T(1,128)}, u32[]{:S(2)}) copy-start(s32[4,1,4]{2,1,0:T(1,128)} %count_ref.1) | copy-start | bytes 196
  2.7 6.3 %collective-permute-start = (bf16[128,256]{1,0:T(8,128)(2,1)S(1)}, bf16[128,256]{1,0:T(8,128)(2,1)S(1)}, u32[]{:S(2)}, u32[]{:S(2)}) collective-permute-start(bf16[128,256]{1,0:T(8,128)(2,1)S(1)} %get-tuple-element.22), channel_id=1, source_target_pairs={{0,8},{8,0},{16,24},{24,16},{1,9},{9,1},{17,25},{25,17},{2,10},{10... | collective-permute-start | bytes 196616 | tf_op jit(solution)/shard_map/ppermute | solution.py:294
  5.8 7.3 %collective-permute-start.1 = (bf16[128,256]{1,0:T(8,128)(2,1)S(1)}, bf16[128,256]{1,0:T(8,128)(2,1)S(1)}, u32[]{:S(2)}, u32[]{:S(2)}) collective-permute-start(bf16[128,256]{1,0:T(8,128)(2,1)S(1)} %get-tuple-element.23), channel_id=1, source_target_pairs={{0,16},{8,24},{16,0},{24,8},{1,17},{9,25},{17,1},{25,9},{2,18},{10... | collective-permute-start | bytes 196616 | tf_op jit(solution)/shard_map/ppermute | solution.py:294
  8.4 6.1 %collective-permute-start.2 = (bf16[128,256]{1,0:T(8,128)(2,1)S(1)}, bf16[128,256]{1,0:T(8,128)(2,1)S(1)}, u32[]{:S(2)}, u32[]{:S(2)}) collective-permute-start(bf16[128,256]{1,0:T(8,128)(2,1)S(1)} %get-tuple-element.24), channel_id=1, source_target_pairs={{0,24},{8,16},{16,8},{24,0},{1,25},{9,17},{17,9},{25,1},{2,26},{10... | collective-permute-start | bytes 196616 | tf_op jit(solution)/shard_map/ppermute | solution.py:294
  14.8 9.0 %copy-start.3 = (f32[3]{0:T(128)S(1)}, f32[3]{0:T(128)}, u32[]{:S(2)}) copy-start(f32[3]{0:T(128)} %param.7) | copy-start | bytes 40
  14.8 3.9 %collective-permute-start.4 = (f32[6,8,128]{2,1,0:T(8,128)S(1)}, f32[6,8,128]{2,1,0:T(8,128)S(1)}, u32[]{:S(2)}, u32[]{:S(2)}) collective-permute-start(f32[6,8,128]{2,1,0:T(8,128)S(1)} %pair_first.1.refs_0_), channel_id=1, source_target_pairs={{0,2},{1,3},{2,0},{3,1},{4,6},{5,7},{6,4},{7,5},{8,10},{9,11},{10,... | collective-permute-start | bytes 73736 | tf_op jit(solution)/shard_map/ppermute | solution.py:285
  16.4 3.8 %collective-permute-start.6 = (f32[6,8,128]{2,1,0:T(8,128)S(1)}, f32[6,8,128]{2,1,0:T(8,128)S(1)}, u32[]{:S(2)}, u32[]{:S(2)}) collective-permute-start(f32[6,8,128]{2,1,0:T(8,128)S(1)} %pair_first.1.refs_0_), channel_id=1, source_target_pairs={{0,4},{1,5},{2,6},{3,7},{4,0},{5,1},{6,2},{7,3},{8,12},{9,13},{10,... | collective-permute-start | bytes 73736 | tf_op jit(solution)/shard_map/ppermute | solution.py:285
  17.9 4.7 %collective-permute-start.8 = (f32[6,8,128]{2,1,0:T(8,128)S(1)}, f32[6,8,128]{2,1,0:T(8,128)S(1)}, u32[]{:S(2)}, u32[]{:S(2)}) collective-permute-start(f32[6,8,128]{2,1,0:T(8,128)S(1)} %pair_first.1.refs_0_), channel_id=1, source_target_pairs={{0,6},{1,7},{2,4},{3,5},{4,2},{5,3},{6,0},{7,1},{8,14},{9,15},{10,... | collective-permute-start | bytes 73736 | tf_op jit(solution)/shard_map/ppermute | solution.py:285
  18.4 4.2 %collective-permute-start.3 = (f32[6,8,128]{2,1,0:T(8,128)S(1)}, f32[6,8,128]{2,1,0:T(8,128)S(1)}, u32[]{:S(2)}, u32[]{:S(2)}) collective-permute-start(f32[6,8,128]{2,1,0:T(8,128)S(1)} %pair_first.1.refs_0_), channel_id=1, source_target_pairs={{0,1},{1,0},{2,3},{3,2},{4,5},{5,4},{6,7},{7,6},{8,9},{9,8},{10,11... | collective-permute-start | bytes 73736 | tf_op jit(solution)/shard_map/ppermute | solution.py:288
  18.7 3.9 %collective-permute-start.5 = (f32[6,8,128]{2,1,0:T(8,128)S(1)}, f32[6,8,128]{2,1,0:T(8,128)S(1)}, u32[]{:S(2)}, u32[]{:S(2)}) collective-permute-start(f32[6,8,128]{2,1,0:T(8,128)S(1)} %collective-permute-done.4.refs_2_), channel_id=1, source_target_pairs={{0,1},{1,0},{2,3},{3,2},{4,5},{5,4},{6,7},{7,6},{8,9},{9,8},{10,11... | collective-permute-start | bytes 73736 | tf_op jit(solution)/shard_map/ppermute | solution.py:288
  20.2 2.4 %collective-permute-start.7 = (f32[6,8,128]{2,1,0:T(8,128)S(1)}, f32[6,8,128]{2,1,0:T(8,128)S(1)}, u32[]{:S(2)}, u32[]{:S(2)}) collective-permute-start(f32[6,8,128]{2,1,0:T(8,128)S(1)} %collective-permute-done.6.refs_4_), channel_id=1, source_target_pairs={{0,1},{1,0},{2,3},{3,2},{4,5},{5,4},{6,7},{7,6},{8,9},{9,8},{10,11... | collective-permute-start | bytes 73736 | tf_op jit(solution)/shard_map/ppermute | solution.py:288
  22.6 1.2 %collective-permute-start.9 = (f32[6,8,128]{2,1,0:T(8,128)S(1)}, f32[6,8,128]{2,1,0:T(8,128)S(1)}, u32[]{:S(2)}, u32[]{:S(2)}) collective-permute-start(f32[6,8,128]{2,1,0:T(8,128)S(1)} %collective-permute-done.8.refs_6_), channel_id=1, source_target_pairs={{0,1},{1,0},{2,3},{3,2},{4,5},{5,4},{6,7},{7,6},{8,9},{9,8},{10,11... | collective-permute-start | bytes 73736 | tf_op jit(solution)/shard_map/ppermute | solution.py:288
  24.5 5.0 %collective-permute-start.10 = (f32[3,8,128]{2,1,0:T(8,128)S(1)}, f32[3,8,128]{2,1,0:T(8,128)S(1)}, u32[]{:S(2)}, u32[]{:S(2)}) collective-permute-start(f32[3,8,128]{2,1,0:T(8,128)S(1)} %solve_first.1.fields_ref.before_ref), channel_id=1, source_target_pairs={{0,8},{8,0},{16,24},{24,16},{1,9},{9,1},{17,25},{25,17},{2,10},{10... | collective-permute-start | bytes 36872 | tf_op jit(solution)/shard_map/ppermute | solution.py:294
  24.6 4.9 %collective-permute-start.11 = (f32[3,8,128]{2,1,0:T(8,128)S(1)}, f32[3,8,128]{2,1,0:T(8,128)S(1)}, u32[]{:S(2)}, u32[]{:S(2)}) collective-permute-start(f32[3,8,128]{2,1,0:T(8,128)S(1)} %solve_first.1.fields_ref.before_ref), channel_id=1, source_target_pairs={{0,16},{8,24},{16,0},{24,8},{1,17},{9,25},{17,1},{25,9},{2,18},{10... | collective-permute-start | bytes 36872 | tf_op jit(solution)/shard_map/ppermute | solution.py:294
  26.9 5.5 %collective-permute-start.12 = (f32[3,8,128]{2,1,0:T(8,128)S(1)}, f32[3,8,128]{2,1,0:T(8,128)S(1)}, u32[]{:S(2)}, u32[]{:S(2)}) collective-permute-start(f32[3,8,128]{2,1,0:T(8,128)S(1)} %solve_first.1.fields_ref.before_ref), channel_id=1, source_target_pairs={{0,24},{8,16},{16,8},{24,0},{1,25},{9,17},{17,9},{25,1},{2,26},{10... | collective-permute-start | bytes 36872 | tf_op jit(solution)/shard_map/ppermute | solution.py:294
  32.8 3.9 %collective-permute-start.14 = (f32[6,8,128]{2,1,0:T(8,128)S(1)}, f32[6,8,128]{2,1,0:T(8,128)S(1)}, u32[]{:S(2)}, u32[]{:S(2)}) collective-permute-start(f32[6,8,128]{2,1,0:T(8,128)S(1)} %pair_next.1.refs_0_), channel_id=1, source_target_pairs={{0,2},{1,3},{2,0},{3,1},{4,6},{5,7},{6,4},{7,5},{8,10},{9,11},{10,... | collective-permute-start | bytes 73736 | tf_op jit(solution)/shard_map/ppermute | solution.py:285
  33.4 3.8 %collective-permute-start.16 = (f32[6,8,128]{2,1,0:T(8,128)S(1)}, f32[6,8,128]{2,1,0:T(8,128)S(1)}, u32[]{:S(2)}, u32[]{:S(2)}) collective-permute-start(f32[6,8,128]{2,1,0:T(8,128)S(1)} %pair_next.1.refs_0_), channel_id=1, source_target_pairs={{0,4},{1,5},{2,6},{3,7},{4,0},{5,1},{6,2},{7,3},{8,12},{9,13},{10,... | collective-permute-start | bytes 73736 | tf_op jit(solution)/shard_map/ppermute | solution.py:285
  33.9 4.7 %collective-permute-start.18 = (f32[6,8,128]{2,1,0:T(8,128)S(1)}, f32[6,8,128]{2,1,0:T(8,128)S(1)}, u32[]{:S(2)}, u32[]{:S(2)}) collective-permute-start(f32[6,8,128]{2,1,0:T(8,128)S(1)} %pair_next.1.refs_0_), channel_id=1, source_target_pairs={{0,6},{1,7},{2,4},{3,5},{4,2},{5,3},{6,0},{7,1},{8,14},{9,15},{10,... | collective-permute-start | bytes 73736 | tf_op jit(solution)/shard_map/ppermute | solution.py:285
  36.3 2.3 %collective-permute-start.13 = (f32[6,8,128]{2,1,0:T(8,128)S(1)}, f32[6,8,128]{2,1,0:T(8,128)S(1)}, u32[]{:S(2)}, u32[]{:S(2)}) collective-permute-start(f32[6,8,128]{2,1,0:T(8,128)S(1)} %pair_next.1.refs_0_), channel_id=1, source_target_pairs={{0,1},{1,0},{2,3},{3,2},{4,5},{5,4},{6,7},{7,6},{8,9},{9,8},{10,11... | collective-permute-start | bytes 73736 | tf_op jit(solution)/shard_map/ppermute | solution.py:288
  36.6 2.0 %collective-permute-start.15 = (f32[6,8,128]{2,1,0:T(8,128)S(1)}, f32[6,8,128]{2,1,0:T(8,128)S(1)}, u32[]{:S(2)}, u32[]{:S(2)}) collective-permute-start(f32[6,8,128]{2,1,0:T(8,128)S(1)} %collective-permute-done.14.refs_2_), channel_id=1, source_target_pairs={{0,1},{1,0},{2,3},{3,2},{4,5},{5,4},{6,7},{7,6},{8,9},{9,8},{10,11... | collective-permute-start | bytes 73736 | tf_op jit(solution)/shard_map/ppermute | solution.py:288
  37.2 1.4 %collective-permute-start.17 = (f32[6,8,128]{2,1,0:T(8,128)S(1)}, f32[6,8,128]{2,1,0:T(8,128)S(1)}, u32[]{:S(2)}, u32[]{:S(2)}) collective-permute-start(f32[6,8,128]{2,1,0:T(8,128)S(1)} %collective-permute-done.16.refs_4_), channel_id=1, source_target_pairs={{0,1},{1,0},{2,3},{3,2},{4,5},{5,4},{6,7},{7,6},{8,9},{9,8},{10,11... | collective-permute-start | bytes 73736 | tf_op jit(solution)/shard_map/ppermute | solution.py:288
  38.6 1.2 %collective-permute-start.19 = (f32[6,8,128]{2,1,0:T(8,128)S(1)}, f32[6,8,128]{2,1,0:T(8,128)S(1)}, u32[]{:S(2)}, u32[]{:S(2)}) collective-permute-start(f32[6,8,128]{2,1,0:T(8,128)S(1)} %collective-permute-done.18.refs_6_), channel_id=1, source_target_pairs={{0,1},{1,0},{2,3},{3,2},{4,5},{5,4},{6,7},{7,6},{8,9},{9,8},{10,11... | collective-permute-start | bytes 73736 | tf_op jit(solution)/shard_map/ppermute | solution.py:288
  (1 other events, 0.7 us)
